TPU v7x, 256 devices: a whole 4x4x8 slice. The times are simulated.
256 devices in a mesh: gx: 16 (over z_hi, x), gy: 16 (over y, z_lo, core).
Axes of the slice: x: 4, y: 4, z: 8 (z_hi: 4, z_lo: 2; z = z_hi * 2 + z_lo), core: 2. Of those that a mesh axis runs over, the one named last changes fastest.
Arguments:
- profiles: float32 [2, 262144, 128], P(None, ('gx', 'gy')), may hold values from 0.5 to 2
- radial: float32 [2, 128, 128], replicated, may hold values from -1 to 2
- rate_const: float32 [262144], P(('gx', 'gy')), may hold values from 0.02 to 0.2
- transfer_coef: float32 [262144], P(('gx', 'gy')), may hold values from 0.1 to 0.5
- live_count: int32 [256], P(('gx', 'gy')), may hold values from 256 to 1024, as said below
- send_lists: int32 [2048, 128], P(('gx', 'gy')), may hold values from 0 to 1023, as said below
- cell_index: int32 [262144], P(('gx', 'gy')), may hold values from 0 to 131071
- contact_cols: int32 [2048, 4], P(('gx', 'gy')), may hold values from 0 to 15, as said below
- contact_blocks: float32 [2048, 4, 128, 128], P(('gx', 'gy')), may hold values from 0 to 0.006
- populations: float32 [7, 512, 512, 128], P(None, 'gx', 'gy'), may hold values from -1.8 to 1.8
Outputs:
- profiles_out: float32 [2, 262144, 128], P(None, ('gx', 'gy'))
- populations_out: float32 [7, 512, 512, 128], P(None, 'gx', 'gy')
Inputs may be any that keep to these rules, and one draw needn't show every extreme that they name: `live_count`: each tile's count is a multiple of 128, at least a quarter of its slots, and some tile is full. `send_lists`: every entry names a live slot of the sending tile. `contact_cols`: blocks 0 to 7 are the tile's own, block 8 + n is ghost block n; every ghost block is named by some row block.
All inputs are finite; a program needn't handle non-finite values.
Results may differ from a plain program's by a relative error of at most 0.0001.
Values sent between devices are 32-bit elements; how exact they have to be, the bound alone decides.
No kernel may reach another device: no remote copies, remote signals or barrier semaphores. Data moves between devices by JAX's collectives and lax.ppermute only.
A program may use at most 128 MiB of HBM per device.

v0:
```python
import functools

import jax
import jax.numpy as jnp
from jax import lax
from jax.experimental import pallas as pl
from jax.experimental.pallas import tpu as pltpu
from jax.sharding import PartitionSpec as P

NR = 128
BLK = 128
SHELL = 16
STEPS = 3
PB = 8
SLOTS = PB * BLK
CX = 32
CELLS = 1024
F32 = jnp.float32
BF16 = jnp.bfloat16

OFFSETS = ((-1, -1), (-1, 0), (-1, 1), (0, -1), (0, 1), (1, -1), (1, 0), (1, 1))
NT = (((1,), (1,)), ((), ()))
NN = (((1,), (0,)), ((), ()))
VM = pl.BlockSpec(memory_space=pltpu.VMEM)
SM = pl.BlockSpec(memory_space=pltpu.SMEM)
ANY = pl.BlockSpec(memory_space=pl.ANY)
PARAMS = pltpu.CompilerParams(vmem_limit_bytes=30 * 1024 * 1024)


def dot(a, b, dims=NN):
    return lax.dot_general(a, b, dims, preferred_element_type=F32)


def split2(x):
    hi = x.astype(BF16)
    return hi, (x - hi.astype(F32)).astype(BF16)


def split3(x):
    hi = x.astype(BF16)
    rest = x - hi.astype(F32)
    mid = rest.astype(BF16)
    return hi, mid, (rest - mid.astype(F32)).astype(BF16)


def flag(cond):
    return jnp.where(cond, 1.0, 0.0).astype(F32)


def pair(ref, j):
    return jnp.concatenate([ref[2 * j : 2 * j + 1, :], ref[2 * j + 1 : 2 * j + 2, :]], axis=1)


def send_part(theta, edge, tt, cell, coef, blocks, ot, slt, thl, vt, source, ex, xu, xd, yu, yd):
    for b in range(PB):
        hi, lo = split2(theta[b * BLK : (b + 1) * BLK, :].T)
        thl[0:128, b * BLK : (b + 1) * BLK] = hi
        thl[128:256, b * BLK : (b + 1) * BLK] = lo
    sub = lax.broadcasted_iota(jnp.int32, (128, 256), 0)
    for j in range(4):
        at = slice(j * 256, (j + 1) * 256)
        g = dot(thl[...], ot[:, at])
        mask = sub == (pair(cell, j) & 127)
        there = jnp.sum(jnp.where(mask, g[0:128, :] + g[128:256, :], 0.0), axis=0, keepdims=True)
        alive = jnp.concatenate(
            [jnp.full((1, 128), flag(2 * j + h < blocks), F32) for h in range(2)], axis=1
        )
        e = pair(coef, j) * (there - tt[15:16, at]) * alive
        ex[2 * j : 2 * j + 1, :] = e[:, 0:128]
        ex[2 * j + 1 : 2 * j + 2, :] = e[:, 128:256]
        hi, lo = split2(jnp.where(mask, e, 0.0))
        vt[0:128, at] = hi
        vt[128:256, at] = lo
    for j in range(4):
        at = slice(j * 256, (j + 1) * 256)
        g = dot(ot[at, :], vt[...], NT)
        source[at, :] = 1.25 * theta[at, :] - 0.5 * (g[:, 0:128] + g[:, 128:256])
    xu[48:80, :] = 0.125 * source[992:1024, :] - 0.25 * edge[0]
    xd[48:80, :] = 0.125 * source[0:32, :] - 0.25 * edge[1]
    yu[16:48, :] = 0.125 * source[pl.ds(31, 32, stride=32), :] - 0.25 * edge[2]
    yd[16:48, :] = 0.125 * source[pl.ds(0, 32, stride=32), :] - 0.25 * edge[3]
    rows = jnp.concatenate(split3(tt[...]), axis=0)
    places = ((xd, 0), (xd, 16), (xd, 32), (yd, 0), (yu, 0), (xu, 0), (xu, 16), (xu, 32))
    for j in range(4):
        g = dot(rows, slt[:, j * 256 : (j + 1) * 256])
        g = g[0:16, :] + g[16:32, :] + g[32:48, :]
        for h in range(2):
            ref, start = places[2 * j + h]
            ref[start : start + 16, :] = g[:, h * 128 : (h + 1) * 128]


def first_kernel(
    live, cell, coef, lists, profiles, pops, ot, slt, tt, source, ex, xu, xd, yu, yd, theta, edge, thl, vt
):
    blocks = live[0] // BLK
    sub = lax.broadcasted_iota(jnp.int32, (CELLS, BLK), 0)
    for b in range(PB):
        at = slice(b * BLK, (b + 1) * BLK)
        ot[:, at] = jnp.where(sub == (cell[b : b + 1, :] >> 7), 1.0, 0.0).astype(BF16)
        slt[:, at] = jnp.where(sub == lists[b : b + 1, :], 1.0, 0.0).astype(BF16)
        tt[:, at] = profiles[0, at, :].T[NR - SHELL :, :]

    def row(x, _):
        at = pl.ds(pl.multiple_of(x * 32, 32), 32)
        total = pops[0, at, :]
        for i in range(1, 7):
            total = total + pops[i, at, :]
        theta[at, :] = total
        return 0

    lax.fori_loop(0, CX, row, 0)
    edge[0] = pops[1, 992:1024, :]
    edge[1] = pops[2, 0:32, :]
    edge[2] = pops[3, pl.ds(31, 32, stride=32), :]
    edge[3] = pops[4, pl.ds(0, 32, stride=32), :]
    send_part(theta, edge, tt, cell, coef, blocks, ot, slt, thl, vt, source, ex, xu, xd, yu, yd)


def stream_kernel(last, n_faces, *refs):
    faces, refs = refs[:n_faces], refs[n_faces:]
    if last:
        pops, source, new, strip3, strip4 = refs
    else:
        pops, source, new, theta, edge = refs
    y = lax.broadcasted_iota(jnp.int32, (32, 128), 0)
    z = lax.broadcasted_iota(jnp.int32, (32, 128), 1)

    def row(x, _):
        at = pl.ds(pl.multiple_of(x * 32, 32), 32)
        before = pl.ds(pl.multiple_of(jnp.maximum(x - 1, 0) * 32, 32), 32)
        after = pl.ds(pl.multiple_of(jnp.minimum(x + 1, CX - 1) * 32, 32), 32)
        s = 0.125 * source[at, :]
        n0 = 2.0 * s - 0.25 * pops[0, at, :]
        new[0, at, :] = n0
        n1 = flag(x > 0) * (0.125 * source[before, :] - 0.25 * pops[1, before, :])
        new[1, at, :] = n1
        n2 = flag(x < CX - 1) * (0.125 * source[after, :] - 0.25 * pops[2, after, :])
        new[2, at, :] = n2
        n3 = jnp.where(y == 0, 0.0, pltpu.roll(s - 0.25 * pops[3, at, :], 1, 0))
        new[3, at, :] = n3
        n4 = jnp.where(y == 31, 0.0, pltpu.roll(s - 0.25 * pops[4, at, :], 31, 0))
        new[4, at, :] = n4
        n5 = jnp.where(z == 0, 0.0, pltpu.roll(s - 0.25 * pops[5, at, :], 1, 1))
        new[5, at, :] = n5
        n6 = jnp.where(z == 127, 0.0, pltpu.roll(s - 0.25 * pops[6, at, :], 127, 1))
        new[6, at, :] = n6
        if not last:
            theta[at, :] = ((n0 + n1) + (n2 + n3)) + ((n4 + n5) + n6)
        return 0

    lax.fori_loop(0, CX, row, 0, unroll=2)
    if n_faces:
        meta, xu, xd, yu, yd = faces
        parts = (
            (1, slice(32, 64), 6, xu[48:80, :]),
            (2, slice(960, 992), 1, xd[48:80, :]),
            (3, pl.ds(1, 32, stride=32), 4, yu[16:48, :]),
            (4, pl.ds(30, 32, stride=32), 3, yd[16:48, :]),
        )
        for i, at, place, face in parts:
            face = face * (-0.25 * meta[place].astype(F32))
            new[i, at, :] = new[i, at, :] + face
            if not last:
                theta[at, :] = theta[at, :] + face
    if last:
        for x in range(CX):
            strip3[x] = new[3, x * 32 : x * 32 + 8, :]
            strip4[x] = new[4, x * 32 + 24 : x * 32 + 32, :]
    else:
        edge[0] = new[1, 992:1024, :]
        edge[1] = new[2, 0:32, :]
        edge[2] = new[3, pl.ds(31, 32, stride=32), :]
        edge[3] = new[4, pl.ds(0, 32, stride=32), :]


def prepare_kernel(rate, blocks, rc, halves):
    for b in range(PB):
        rc[b * BLK : (b + 1) * BLK, :] = jnp.broadcast_to(rate[b : b + 1, :], (BLK, NR)).T
        for k in range(4):
            hi, lo = split2(blocks[b, k])
            halves[b, k, :, 0:128] = hi
            halves[b, k, :, 128:256] = lo


def mix_part(blocks, temp_of, conc_of, radial, rc, base, conc_new):
    wide = []
    for c in range(2):
        hi, lo = split2(radial[c])
        wide.append(
            jnp.concatenate(
                [jnp.concatenate([hi, lo], axis=1), jnp.concatenate([hi, jnp.zeros_like(hi)], axis=1)],
                axis=0,
            )
        )
    for b in range(PB):
        at = slice(b * BLK, (b + 1) * BLK)
        temp, conc = temp_of(at), conc_of(at)
        alive = flag(b < blocks)
        rate = rc[at, :] * conc * jnp.exp(0.5 * jnp.tanh(temp - 1.0))
        g = dot(jnp.concatenate(split2(temp), axis=1), wide[0])
        base[at, :] = (g[:, 0:128] + g[:, 128:256]) + rate
        g = dot(jnp.concatenate(split2(conc), axis=1), wide[1])
        conc_new[at, :] = alive * ((g[:, 0:128] + g[:, 128:256]) - rate) + (1.0 - alive) * conc


def mix_first_kernel(live, profiles, radial, rc, base, conc_new):
    mix_part(live[0] // BLK, lambda at: profiles[0, at, :], lambda at: profiles[1, at, :], radial, rc, base, conc_new)


def mix_kernel(live, temp, conc, radial, rc, base, conc_new):
    mix_part(live[0] // BLK, lambda at: temp[at, :], lambda at: conc[at, :], radial, rc, base, conc_new)


def contact_part(live_blocks, meta, cols, temp_of, base, ex, tt, halves, rxu, rxd, ryu, ryd, extended, store):
    for b in range(PB):
        alive = flag(b < live_blocks)
        hi, lo = split2(tt[:, b * BLK : (b + 1) * BLK] * alive)
        extended[b, 0:16, :] = hi
        extended[b, 16:32, :] = lo
        extended[b, 32:48, :] = jnp.full((16, 128), alive, F32).astype(BF16)
    places = ((ryd, 48), (rxd, 16), (ryu, 48), (ryd, 0), (ryu, 0), (ryd, 64), (rxu, 16), (ryu, 64))
    for n in range(8):
        ref, start = places[n]
        there = meta[n].astype(F32)
        hi, lo = split2(ref[start : start + 16, :] * there)
        extended[8 + n, 0:16, :] = hi
        extended[8 + n, 16:32, :] = lo
        extended[8 + n, 32:48, :] = jnp.full((16, 128), there, F32).astype(BF16)
    row = lax.broadcasted_iota(jnp.int32, (16, 128), 0)
    for b in range(PB):
        at = slice(b * BLK, (b + 1) * BLK)
        total = None
        for k in range(4):
            x = extended[cols[b, k]]
            g = dot(jnp.concatenate([x, x], axis=1), halves[b, k], NT)
            total = g if total is None else total + g
        flow = total[0:16, :] + total[16:32, :] - total[32:33, :] * tt[:, at]
        flow = jnp.where(row == 15, flow + ex[b : b + 1, :], flow)
        added = jnp.concatenate([jnp.zeros((NR - SHELL, BLK), F32), flow], axis=0).T
        alive = flag(b < live_blocks)
        store(b, at, alive * (base[at, :] + added) + (1.0 - alive) * temp_of(at))


def middle_kernel(
    temp_3d, live, meta, cols, temp, base, ex_in, tt_in, halves, rxu, rxd, ryu, ryd,
    theta_in, edge, cell, coef, ot, slt,
    temp_out, tt, source, ex, xu, xd, yu, yd, extended, theta, thl, vt,
):
    blocks = live[0] // BLK

    def store(b, at, value):
        temp_out[at, :] = value
        tt[:, at] = value.T[NR - SHELL :, :]

    old = (lambda at: temp[0, at, :]) if temp_3d else (lambda at: temp[at, :])
    contact_part(blocks, meta, cols, old, base, ex_in, tt_in, halves, rxu, rxd, ryu, ryd, extended, store)
    theta[...] = theta_in[...]
    for at, place, face in (
        (slice(0, 32), 6, rxu[48:80, :]),
        (slice(992, 1024), 1, rxd[48:80, :]),
        (pl.ds(0, 32, stride=32), 4, ryu[16:48, :]),
        (pl.ds(31, 32, stride=32), 3, ryd[16:48, :]),
    ):
        theta[at, :] = theta[at, :] + face * meta[place].astype(F32)
    send_part(theta, edge, tt, cell, coef, blocks, ot, slt, thl, vt, source, ex, xu, xd, yu, yd)


def last_kernel(
    live, meta, cols, temp, base, conc, ex_in, tt_in, halves, rxu, rxd, ryu, ryd, strip3, strip4, pops_in,
    profiles, pops, extended, face1, face2, patch3, patch4, sems,
):
    face1[...] = rxu[48:80, :] * meta[6].astype(F32)
    face2[...] = rxd[48:80, :] * meta[1].astype(F32)
    y = lax.broadcasted_iota(jnp.int32, (8, 128), 0)
    for x in range(CX):
        patch3[x] = jnp.where(y == 0, ryu[16 + x : 17 + x, :] * meta[4].astype(F32), strip3[x])
        patch4[x] = jnp.where(y == 7, ryd[16 + x : 17 + x, :] * meta[3].astype(F32), strip4[x])
    copies = [
        pltpu.make_async_copy(face1, pops.at[1, 0], sems.at[0]),
        pltpu.make_async_copy(face2, pops.at[2, CX - 1], sems.at[1]),
        pltpu.make_async_copy(patch3, pops.at[3, :, 0:8, :], sems.at[2]),
        pltpu.make_async_copy(patch4, pops.at[4, :, 24:32, :], sems.at[3]),
    ]
    for c in copies:
        c.start()

    def store(b, at, value):
        profiles[0, at, :] = value
        profiles[1, at, :] = conc[at, :]

    old = lambda at: temp[at, :]
    contact_part(
        live[0] // BLK, meta, cols, old, base, ex_in, tt_in, halves, rxu, rxd, ryu, ryd, extended, store
    )
    for c in copies:
        c.wait()


def call(kernel, name, ins, in_specs, outs, out_specs=None, scratch=(), us=2, aliases=None):
    shapes = [jax.ShapeDtypeStruct(s, d) for s, d in outs]
    return pl.pallas_call(
        kernel,
        name=name,
        out_shape=shapes,
        in_specs=in_specs,
        out_specs=[VM] * len(outs) if out_specs is None else out_specs,
        scratch_shapes=list(scratch),
        compiler_params=PARAMS,
        input_output_aliases=aliases or {},
        cost_estimate=pl.CostEstimate(flops=us * 10**8, bytes_accessed=us * 3 * 10**6, transcendentals=0),
    )(*ins)


def exchange_x(xu, xd):
    n = lax.axis_size("gx")
    up = [(i, (i + 1) % n) for i in range(n)]
    down = [(j, i) for i, j in up]
    return lax.ppermute(xu, "gx", up), lax.ppermute(xd, "gx", down)


def exchange_y(yu, yd, rxu, rxd):
    n = lax.axis_size("gy")
    up = [(i, (i + 1) % n) for i in range(n)]
    down = [(j, i) for i, j in up]
    to_up = jnp.concatenate([yu, rxd[32:48], rxu[32:48]], axis=0)
    to_down = jnp.concatenate([yd, rxd[0:16], rxu[0:16]], axis=0)
    return lax.ppermute(to_up, "gy", up), lax.ppermute(to_down, "gy", down)


def on_device(
    profiles, radial, rate_const, transfer_coef, live_count, send_lists, cell_index, contact_cols, contact_blocks, populations
):
    cell = cell_index.reshape(PB, BLK)
    coef = transfer_coef.reshape(PB, BLK)
    rate = rate_const.reshape(PB, BLK)
    pops = populations.reshape(7, CELLS, 128)
    blocks = contact_blocks.reshape(PB, 4, BLK, BLK)
    ix, iy = lax.axis_index("gx"), lax.axis_index("gy")
    nx, ny = lax.axis_size("gx"), lax.axis_size("gy")
    meta = jnp.stack(
        [
            ((ix - a >= 0) & (ix - a < nx) & (iy - b >= 0) & (iy - b < ny)).astype(jnp.int32)
            for a, b in OFFSETS
        ]
    )
    plane = ((SLOTS, 128), F32)
    out_send = [((80, 128), F32)] * 2 + [((48, 128), F32)] * 2
    work = [pltpu.VMEM((256, 1024), BF16), pltpu.VMEM((256, 1024), BF16)]
    theta_s = pltpu.VMEM((CELLS, 128), F32)
    ext_s = pltpu.VMEM((16, 48, 128), BF16)

    ot, slt, tt, source, ex, xu, xd, yu, yd = call(
        first_kernel, "first",
        (live_count, cell, coef, send_lists, profiles, pops), [SM] + [VM] * 5,
        [((CELLS, SLOTS), BF16), ((SLOTS, SLOTS), BF16), ((SHELL, SLOTS), F32), plane, ((PB, BLK), F32)] + out_send,
        scratch=[theta_s, pltpu.VMEM((4, 32, 128), F32)] + work, us=6,
    )
    rc, halves = call(
        prepare_kernel, "prepare", (rate, blocks), [VM, VM], [plane, ((PB, 4, BLK, 256), BF16)]
    )
    temp = conc = received = None
    for step in range(STEPS):
        final = step == STEPS - 1
        rxu, rxd = exchange_x(xu, xd)
        if step == 0:
            base, conc_new = call(
                mix_first_kernel, "mix_first", (live_count, profiles, radial, rc), [SM] + [VM] * 3, [plane, plane]
            )
        else:
            base, conc_new = call(
                mix_kernel, "mix", (live_count, temp, conc, radial, rc), [SM] + [VM] * 4, [plane, plane]
            )
        faces = () if step == 0 else (meta, *received)
        last_outs = [((CX, 8, 128), F32)] * 2 if final else [plane, ((4, 32, 128), F32)]
        streamed = call(
            functools.partial(stream_kernel, final, len(faces)), "stream",
            (*faces, pops, source), [SM] * (step > 0) + [VM] * (6 if step else 2),
            [((7, CELLS, 128), F32)] + last_outs,
        )
        ryu, ryd = exchange_y(yu, yd, rxu, rxd)
        received = (rxu, rxd, ryu, ryd)
        if final:
            whole = streamed[0].reshape(7, CX, 32, 128)
            profiles_out, pops_out = call(
                last_kernel, "last",
                (live_count, meta, contact_cols, temp, base, conc_new, ex, tt, halves, *received, *streamed[1:], whole),
                [SM] * 3 + [VM] * 12 + [ANY],
                [((2, SLOTS, NR), F32), ((7, CX, 32, 128), F32)],
                out_specs=[VM, ANY],
                scratch=[ext_s] + [pltpu.VMEM((32, 128), F32)] * 2 + [pltpu.VMEM((CX, 8, 128), F32)] * 2
                + [pltpu.SemaphoreType.DMA((4,))],
                aliases={15: 1},
            )
            return profiles_out, pops_out
        pops, theta, edge = streamed
        temp, tt, source, ex, xu, xd, yu, yd = call(
            functools.partial(middle_kernel, step == 0), "middle",
            (live_count, meta, contact_cols, profiles if step == 0 else temp, base, ex, tt, halves, *received,
             theta, edge, cell, coef, ot, slt),
            [SM] * 3 + [VM] * 15,
            [plane, ((SHELL, SLOTS), F32), plane, ((PB, BLK), F32)] + out_send,
            scratch=[ext_s, theta_s] + work, us=6,
        )
        conc = conc_new


def solution(mesh):
    return jax.shard_map(
        on_device,
        mesh=mesh,
        in_specs=(
            P(None, ("gx", "gy"), None),
            P(),
            P(("gx", "gy")),
            P(("gx", "gy")),
            P(("gx", "gy")),
            P(("gx", "gy"), None),
            P(("gx", "gy")),
            P(("gx", "gy"), None),
            P(("gx", "gy"), None, None, None),
            P(None, "gx", "gy", None),
        ),
        out_specs=(P(None, ("gx", "gy"), None), P(None, "gx", "gy", None)),
        check_vma=False,
    )
```

profile of v0, /device:TPU:1, one launch (start us, length us, event | category | flops | bytes accessed | tf_op | source)
XLA Modules:
  0.0 80.8 jit_solution(13062339716777796819)
XLA Ops:
  1.3 2.0 %copy-done = f32[7,32,32,128]{3,2,1,0:T(8,128)S(1)} copy-done((f32[7,32,32,128]{3,2,1,0:T(8,128)S(1)}, f32[7,32,32,128]{3,2,1,0:T(8,128)}, u32[]{:S(2)}) %copy-start) | copy-done | bytes 3670040
  3.3 1.2 %copy-done.2 = f32[2,1024,128]{2,1,0:T(8,128)S(1)} copy-done((f32[2,1024,128]{2,1,0:T(8,128)S(1)}, f32[2,1024,128]{2,1,0:T(8,128)}, u32[]{:S(2)}) %copy-start.2) | copy-done | bytes 1048600
  4.5 0.7 copy-done.14
  5.2 0.7 copy-done.16
  5.9 0.7 copy-done.19
  6.6 4.7 %first.1 = (bf16[1024,1024]{1,0:T(8,128)(2,1)S(1)}, bf16[1024,1024]{1,0:T(8,128)(2,1)S(1)}, f32[16,1024]{1,0:T(8,128)S(1)}, f32[1024,128]{1,0:T(8,128)S(1)}, f32...) custom-call(s32[1]{0:T(128)S(6)} %copy.17.live, ...), custom_call_target="tpu_custom_call" | custom-call | flops 600000000 | bytes 18000000 | tf_op jit(solution)/shard_map/first/pallas_call | solution.py:301
  11.3 1.4 %copy-done.4 = bf16[1024,1024]{1,0:T(8,128)(2,1)} copy-done((bf16[1024,1024]{1,0:T(8,128)(2,1)}, bf16[1024,1024]{1,0:T(8,128)(2,1)S(1)}, u32[]{:S(2)}) %copy-start.4) | copy-done | bytes 2097176
  12.6 9.0 %collective-permute-start.1 = (f32[80,128]{1,0:T(8,128)S(1)}, f32[80,128]{1,0:T(8,128)S(1)}, u32[]{:S(2)}, u32[]{:S(2)}) collective-permute-start(f32[80,128]{1,0:T(8,128)S(1)} %get-tuple-element.50), channel_id=1, source_target_pairs={{16,0},{32,16},{48,32},{64,48},{80,64},{96,80},{112,96},{128,112},... | collective-permute-start | bytes 122888 | tf_op jit(solution)/shard_map/ppermute | solution.py:318
  21.7 1.1 %collective-permute-done.1.rxd.refs_2_ = f32[80,128]{1,0:T(8,128)S(1)} collective-permute-done((f32[80,128]{1,0:T(8,128)S(1)}, f32[80,128]{1,0:T(8,128)S(1)}, u32[]{:S(2)}, u32[]{:S(2)}) %collective-permute-start.1) | collective-permute-done | bytes 40992 | tf_op jit(solution)/shard_map/ppermute | solution.py:318
  22.8 6.0 %collective-permute-done.rxu.refs_1_ = f32[80,128]{1,0:T(8,128)S(1)} collective-permute-done((f32[80,128]{1,0:T(8,128)S(1)}, f32[80,128]{1,0:T(8,128)S(1)}, u32[]{:S(2)}, u32[]{:S(2)}) %collective-permute-start) | collective-permute-done | bytes 40992 | tf_op jit(solution)/shard_map/ppermute | solution.py:318
  29.4 2.1 %collective-permute-start.3 = (f32[80,128]{1,0:T(8,128)}, f32[80,128]{1,0:T(8,128)S(1)}, u32[]{:S(2)}, u32[]{:S(2)}) collective-permute-start(f32[80,128]{1,0:T(8,128)} %pad_maximum_fusion.1), channel_id=1, source_target_pairs={{1,0},{2,1},{3,2},{4,3},{5,4},{6,5},{7,6},{8,7},{9,8},{10,9},{11,1... | collective-permute-start | bytes 122888 | tf_op jit(solution)/shard_map/ppermute | solution.py:327
  31.5 0.6 pad_maximum_fusion
  32.1 0.6 collective-permute-start.2
  32.7 1.5 %stream.3 = (f32[7,1024,128]{2,1,0:T(8,128)S(1)}, f32[1024,128]{1,0:T(8,128)S(1)}, f32[4,32,128]{2,1,0:T(8,128)S(1)}) custom-call(f32[7,1024,128]{2,1,0:T(8,128)S(1)} %bitcast.14, f32[1024,128]{1,0:T(8,128)S(1)} %get-tuple-element.53.refs_1_), custom_call_target="tpu_custom_call" | custom-call | flops 200000000 | bytes 6000000 | tf_op jit(solution)/shard_map/stream/pallas_call | solution.py:301
  34.2 1.8 %copy-done.6 = f32[7,1024,128]{2,1,0:T(8,128)} copy-done((f32[7,1024,128]{2,1,0:T(8,128)}, f32[7,1024,128]{2,1,0:T(8,128)S(1)}, u32[]{:S(2)}) %copy-start.6) | copy-done | bytes 3670040
  36.1 0.8 copy-done.10
  36.9 0.6 copy-done.12
  37.7 1.7 %copy-done.8 = f32[8,4,128,128]{3,2,1,0:T(8,128)S(1)} copy-done((f32[8,4,128,128]{3,2,1,0:T(8,128)S(1)}, f32[8,4,128,128]{3,2,1,0:T(8,128)}, u32[]{:S(2)}) %copy-start.8) | copy-done | bytes 2097176
  40.6 3.0 %middle.2 = (f32[1024,128]{1,0:T(8,128)S(1)}, f32[16,1024]{1,0:T(8,128)S(1)}, f32[1024,128]{1,0:T(8,128)S(1)}, f32[8,128]{1,0:T(8,128)S(1)}, f32[80,128]{1,0:T(8...) custom-call(s32[1]{0:T(128)S(6)} %copy.17.live, s32[8]{0:T(128)S(1)} %stack.46.meta.refs_0_, ...), custom_call_target="tpu_custom_call" | custom-call | flops 600000000 | bytes 18000000 | tf_op jit(solution)/shard_map/middle/pallas_call | solution.py:301
  43.6 1.5 %collective-permute-start.4 = (f32[80,128]{1,0:T(8,128)S(1)}, f32[80,128]{1,0:T(8,128)S(1)}, u32[]{:S(2)}, u32[]{:S(2)}) collective-permute-start(f32[80,128]{1,0:T(8,128)S(1)} %get-tuple-element.63), channel_id=1, source_target_pairs={{0,16},{16,32},{32,48},{48,64},{64,80},{80,96},{96,112},{112,128},... | collective-permute-start | bytes 122888 | tf_op jit(solution)/shard_map/ppermute | solution.py:318
  45.1 1.4 %collective-permute-done.5.rxd.refs_2_ = f32[80,128]{1,0:T(8,128)S(1)} collective-permute-done((f32[80,128]{1,0:T(8,128)S(1)}, f32[80,128]{1,0:T(8,128)S(1)}, u32[]{:S(2)}, u32[]{:S(2)}) %collective-permute-start.5) | collective-permute-done | bytes 40992 | tf_op jit(solution)/shard_map/ppermute | solution.py:318
  46.5 4.4 %collective-permute-done.4.rxu.refs_1_ = f32[80,128]{1,0:T(8,128)S(1)} collective-permute-done((f32[80,128]{1,0:T(8,128)S(1)}, f32[80,128]{1,0:T(8,128)S(1)}, u32[]{:S(2)}, u32[]{:S(2)}) %collective-permute-start.4) | collective-permute-done | bytes 40992 | tf_op jit(solution)/shard_map/ppermute | solution.py:318
  50.9 2.1 %collective-permute-start.7 = (f32[80,128]{1,0:T(8,128)S(1)}, f32[80,128]{1,0:T(8,128)S(1)}, u32[]{:S(2)}, u32[]{:S(2)}) collective-permute-start(f32[80,128]{1,0:T(8,128)S(1)} %pad_maximum_fusion.3), channel_id=1, source_target_pairs={{1,0},{2,1},{3,2},{4,3},{5,4},{6,5},{7,6},{8,7},{9,8},{10,9},{11,1... | collective-permute-start | bytes 122888 | tf_op jit(solution)/shard_map/ppermute | solution.py:327
  53.9 2.1 %stream.4 = (f32[7,1024,128]{2,1,0:T(8,128)S(1)}, f32[1024,128]{1,0:T(8,128)S(1)}, f32[4,32,128]{2,1,0:T(8,128)S(1)}) custom-call(s32[8]{0:T(128)S(1)} %stack.46.meta.refs_0_, f32[80,128]{1,0:T(8,128)S(1)} %collective-permute-done.rxu.refs_1_, f32[80,128]{1,0:T(8,128)S(1)} %collective-permute-done.1.rxd.refs_2_, ...), custom_call_target="tpu_custom_call" | custom-call | flops 200000000 | bytes 6000000 | tf_op jit(solution)/shard_map/stream/pallas_call | solution.py:301
  56.0 0.7 collective-permute-done.6.ryu.refs_3_
  56.7 3.0 %middle.3 = (f32[1024,128]{1,0:T(8,128)S(1)}, f32[16,1024]{1,0:T(8,128)S(1)}, f32[1024,128]{1,0:T(8,128)S(1)}, f32[8,128]{1,0:T(8,128)S(1)}, f32[80,128]{1,0:T(8...) custom-call(s32[1]{0:T(128)S(6)} %copy.17.live, s32[8]{0:T(128)S(1)} %stack.46.meta.refs_0_, ...), custom_call_target="tpu_custom_call" | custom-call | flops 600000000 | bytes 18000000 | tf_op jit(solution)/shard_map/middle/pallas_call | solution.py:301
  59.8 1.5 %collective-permute-start.8 = (f32[80,128]{1,0:T(8,128)S(1)}, f32[80,128]{1,0:T(8,128)S(1)}, u32[]{:S(2)}, u32[]{:S(2)}) collective-permute-start(f32[80,128]{1,0:T(8,128)S(1)} %get-tuple-element.77), channel_id=1, source_target_pairs={{0,16},{16,32},{32,48},{48,64},{64,80},{80,96},{96,112},{112,128},... | collective-permute-start | bytes 122888 | tf_op jit(solution)/shard_map/ppermute | solution.py:318
  61.3 1.4 %collective-permute-done.9.rxd = f32[80,128]{1,0:T(8,128)S(1)} collective-permute-done((f32[80,128]{1,0:T(8,128)S(1)}, f32[80,128]{1,0:T(8,128)S(1)}, u32[]{:S(2)}, u32[]{:S(2)}) %collective-permute-start.9) | collective-permute-done | bytes 40992 | tf_op jit(solution)/shard_map/ppermute | solution.py:318
  62.6 4.3 %collective-permute-done.8.rxu = f32[80,128]{1,0:T(8,128)S(1)} collective-permute-done((f32[80,128]{1,0:T(8,128)S(1)}, f32[80,128]{1,0:T(8,128)S(1)}, u32[]{:S(2)}, u32[]{:S(2)}) %collective-permute-start.8) | collective-permute-done | bytes 40992 | tf_op jit(solution)/shard_map/ppermute | solution.py:318
  67.0 5.9 %collective-permute-start.11 = (f32[80,128]{1,0:T(8,128)S(1)}, f32[80,128]{1,0:T(8,128)S(1)}, u32[]{:S(2)}, u32[]{:S(2)}) collective-permute-start(f32[80,128]{1,0:T(8,128)S(1)} %pad_maximum_fusion.5), channel_id=1, source_target_pairs={{1,0},{2,1},{3,2},{4,3},{5,4},{6,5},{7,6},{8,7},{9,8},{10,9},{11,1... | collective-permute-start | bytes 122888 | tf_op jit(solution)/shard_map/ppermute | solution.py:327
  73.4 4.1 %stream.5 = (f32[7,1024,128]{2,1,0:T(8,128)}, f32[32,8,128]{2,1,0:T(8,128)S(1)}, f32[32,8,128]{2,1,0:T(8,128)S(1)}) custom-call(s32[8]{0:T(128)S(1)} %stack.46.meta.refs_0_, f32[80,128]{1,0:T(8,128)S(1)} %collective-permute-done.4.rxu.refs_1_, f32[80,128]{1,0:T(8,128)S(1)} %collective-permute-done.5.rxd.refs_2_, ...), custom_call_target="tpu_custom_call" | custom-call | flops 200000000 | bytes 6000000 | tf_op jit(solution)/shard_map/stream/pallas_call | solution.py:301
  77.5 3.1 %last.1 = (f32[2,1024,128]{2,1,0:T(8,128)}, f32[7,32,32,128]{3,2,1,0:T(8,128)}) custom-call(s32[1]{0:T(128)S(6)} %copy.17.live, s32[8]{0:T(128)S(1)} %stack.46.meta.refs_0_, s32[8,4]{1,0:T(8,128)S(1)} %copy.15.cols, f32[1024,128]{1,0:T(8,128)S(1)} %get-tuple-element.71.temp, ...), custom_call_target="tpu_custom_call", output_to_operand_aliasing={{1}: (15, {})} | custom-call | flops 200000000 | bytes 6000000 | tf_op jit(solution)/shard_map/last/pallas_call | solution.py:301
  (60 shorter events, 3.3 us)
Async XLA Ops:
  1.3 2.0 %copy-start = (f32[7,32,32,128]{3,2,1,0:T(8,128)S(1)}, f32[7,32,32,128]{3,2,1,0:T(8,128)}, u32[]{:S(2)}) copy-start(f32[7,32,32,128]{3,2,1,0:T(8,128)} %param.19) | copy-start | bytes 11010052
  3.3 1.2 %copy-start.2 = (f32[2,1024,128]{2,1,0:T(8,128)S(1)}, f32[2,1024,128]{2,1,0:T(8,128)}, u32[]{:S(2)}) copy-start(f32[2,1024,128]{2,1,0:T(8,128)} %temp.1) | copy-start | bytes 3145732
  4.5 0.7 copy-start.14
  5.2 0.7 copy-start.16
  5.9 0.7 copy-start.19
  6.6 26.1 %copy-start.1 = (f32[7,32,32,128]{3,2,1,0:T(8,128)S(1)}, f32[7,32,32,128]{3,2,1,0:T(8,128)}, u32[]{:S(2)}) copy-start(f32[7,32,32,128]{3,2,1,0:T(8,128)} %param.19) | copy-start | bytes 11010052
  6.6 31.0 %copy-start.20 = (s32[8,4]{0,1:T(4,128)S(1)}, s32[8,4]{0,1:T(4,128)}, u32[]{:S(2)}) copy-start(s32[8,4]{0,1:T(4,128)} %param.17) | copy-start | bytes 388
  6.6 31.1 %copy-start.18 = (f32[1024]{0:T(1024)S(1)}, f32[1024]{0:T(1024)}, u32[]{:S(2)}) copy-start(f32[1024]{0:T(1024)} %param.12) | copy-start | bytes 12292
  11.3 1.4 %copy-start.4 = (bf16[1024,1024]{1,0:T(8,128)(2,1)}, bf16[1024,1024]{1,0:T(8,128)(2,1)S(1)}, u32[]{:S(2)}) copy-start(bf16[1024,1024]{1,0:T(8,128)(2,1)S(1)} %get-tuple-element.57.slt) | copy-start | bytes 6291460
  12.6 27.3 %copy-start.3 = (f32[2,1024,128]{2,1,0:T(8,128)S(1)}, f32[2,1024,128]{2,1,0:T(8,128)}, u32[]{:S(2)}) copy-start(f32[2,1024,128]{2,1,0:T(8,128)} %temp.1) | copy-start | bytes 3145732
  12.6 27.3 %copy-start.9 = (f32[2,128,128]{2,1,0:T(8,128)S(1)}, f32[2,128,128]{2,1,0:T(8,128)}, u32[]{:S(2)}) copy-start(f32[2,128,128]{2,1,0:T(8,128)} %radial.5) | copy-start | bytes 393220
  12.6 10.1 %collective-permute-start.1 = (f32[80,128]{1,0:T(8,128)S(1)}, f32[80,128]{1,0:T(8,128)S(1)}, u32[]{:S(2)}, u32[]{:S(2)}) collective-permute-start(f32[80,128]{1,0:T(8,128)S(1)} %get-tuple-element.50), channel_id=1, source_target_pairs={{16,0},{32,16},{48,32},{64,48},{80,64},{96,80},{112,96},{128,112},... | collective-permute-start | bytes 122888 | tf_op jit(solution)/shard_map/ppermute | solution.py:318
  21.7 7.1 %collective-permute-start = (f32[80,128]{1,0:T(8,128)S(1)}, f32[80,128]{1,0:T(8,128)S(1)}, u32[]{:S(2)}, u32[]{:S(2)}) collective-permute-start(f32[80,128]{1,0:T(8,128)S(1)} %get-tuple-element.49), channel_id=1, source_target_pairs={{0,16},{16,32},{32,48},{48,64},{64,80},{80,96},{96,112},{112,128},... | collective-permute-start | bytes 122888 | tf_op jit(solution)/shard_map/ppermute | solution.py:318
  29.4 11.0 %collective-permute-start.3 = (f32[80,128]{1,0:T(8,128)}, f32[80,128]{1,0:T(8,128)S(1)}, u32[]{:S(2)}, u32[]{:S(2)}) collective-permute-start(f32[80,128]{1,0:T(8,128)} %pad_maximum_fusion.1), channel_id=1, source_target_pairs={{1,0},{2,1},{3,2},{4,3},{5,4},{6,5},{7,6},{8,7},{9,8},{10,9},{11,1... | collective-permute-start | bytes 122888 | tf_op jit(solution)/shard_map/ppermute | solution.py:327
  32.1 8.3 %collective-permute-start.2 = (f32[80,128]{1,0:T(8,128)}, f32[80,128]{1,0:T(8,128)S(1)}, u32[]{:S(2)}, u32[]{:S(2)}) collective-permute-start(f32[80,128]{1,0:T(8,128)} %pad_maximum_fusion), channel_id=1, source_target_pairs={{0,1},{1,2},{2,3},{3,4},{4,5},{5,6},{6,7},{7,8},{8,9},{9,10},{10,1... | collective-permute-start | bytes 122888 | tf_op jit(solution)/shard_map/ppermute | solution.py:327
  32.7 7.7 %copy-start.15 = (s32[1024]{0:T(1024)S(1)}, s32[1024]{0:T(1024)}, u32[]{:S(2)}) copy-start(s32[1024]{0:T(1024)} %param.16) | copy-start | bytes 12292
  32.7 7.7 %copy-start.17 = (f32[1024]{0:T(1024)S(1)}, f32[1024]{0:T(1024)}, u32[]{:S(2)}) copy-start(f32[1024]{0:T(1024)} %param.13) | copy-start | bytes 12292
  34.2 1.8 %copy-start.6 = (f32[7,1024,128]{2,1,0:T(8,128)}, f32[7,1024,128]{2,1,0:T(8,128)S(1)}, u32[]{:S(2)}) copy-start(f32[7,1024,128]{2,1,0:T(8,128)S(1)} %get-tuple-element.67.refs_5_) | copy-start | bytes 11010052
  36.1 0.8 copy-start.10
  37.7 2.8 %copy-start.5 = (bf16[1024,1024]{1,0:T(8,128)(2,1)S(1)}, bf16[1024,1024]{1,0:T(8,128)(2,1)}, u32[]{:S(2)}) copy-start(bf16[1024,1024]{1,0:T(8,128)(2,1)} %copy-done.4) | copy-start | bytes 6291460
  37.7 1.7 %copy-start.8 = (f32[8,4,128,128]{3,2,1,0:T(8,128)S(1)}, f32[8,4,128,128]{3,2,1,0:T(8,128)}, u32[]{:S(2)}) copy-start(f32[8,4,128,128]{3,2,1,0:T(8,128)} %blocks.1) | copy-start | bytes 6291460
  39.4 1.2 %copy-start.11 = (f32[1024,128]{1,0:T(8,128)S(1)}, f32[1024,128]{1,0:T(8,128)}, u32[]{:S(2)}) copy-start(f32[1024,128]{1,0:T(8,128)} %copy-done.10) | copy-start | bytes 1572868
  39.4 1.2 %copy-start.13 = (f32[4,32,128]{2,1,0:T(8,128)S(1)}, f32[4,32,128]{2,1,0:T(8,128)}, u32[]{:S(2)}) copy-start(f32[4,32,128]{2,1,0:T(8,128)} %copy-done.12) | copy-start | bytes 196612
  40.6 13.3 %copy-start.7 = (f32[7,1024,128]{2,1,0:T(8,128)S(1)}, f32[7,1024,128]{2,1,0:T(8,128)}, u32[]{:S(2)}) copy-start(f32[7,1024,128]{2,1,0:T(8,128)} %copy-done.6) | copy-start | bytes 11010052
  43.6 2.9 %collective-permute-start.5 = (f32[80,128]{1,0:T(8,128)S(1)}, f32[80,128]{1,0:T(8,128)S(1)}, u32[]{:S(2)}, u32[]{:S(2)}) collective-permute-start(f32[80,128]{1,0:T(8,128)S(1)} %get-tuple-element.64), channel_id=1, source_target_pairs={{16,0},{32,16},{48,32},{64,48},{80,64},{96,80},{112,96},{128,112},... | collective-permute-start | bytes 122888 | tf_op jit(solution)/shard_map/ppermute | solution.py:318
  43.6 7.2 %collective-permute-start.4 = (f32[80,128]{1,0:T(8,128)S(1)}, f32[80,128]{1,0:T(8,128)S(1)}, u32[]{:S(2)}, u32[]{:S(2)}) collective-permute-start(f32[80,128]{1,0:T(8,128)S(1)} %get-tuple-element.63), channel_id=1, source_target_pairs={{0,16},{16,32},{32,48},{48,64},{64,80},{80,96},{96,112},{112,128},... | collective-permute-start | bytes 122888 | tf_op jit(solution)/shard_map/ppermute | solution.py:318
  50.9 5.1 %collective-permute-start.7 = (f32[80,128]{1,0:T(8,128)S(1)}, f32[80,128]{1,0:T(8,128)S(1)}, u32[]{:S(2)}, u32[]{:S(2)}) collective-permute-start(f32[80,128]{1,0:T(8,128)S(1)} %pad_maximum_fusion.3), channel_id=1, source_target_pairs={{1,0},{2,1},{3,2},{4,3},{5,4},{6,5},{7,6},{8,7},{9,8},{10,9},{11,1... | collective-permute-start | bytes 122888 | tf_op jit(solution)/shard_map/ppermute | solution.py:327
  53.0 3.7 %collective-permute-start.6 = (f32[80,128]{1,0:T(8,128)S(1)}, f32[80,128]{1,0:T(8,128)S(1)}, u32[]{:S(2)}, u32[]{:S(2)}) collective-permute-start(f32[80,128]{1,0:T(8,128)S(1)} %pad_maximum_fusion.2), channel_id=1, source_target_pairs={{0,1},{1,2},{2,3},{3,4},{4,5},{5,6},{6,7},{7,8},{8,9},{9,10},{10,1... | collective-permute-start | bytes 122888 | tf_op jit(solution)/shard_map/ppermute | solution.py:327
  59.8 2.9 %collective-permute-start.9 = (f32[80,128]{1,0:T(8,128)S(1)}, f32[80,128]{1,0:T(8,128)S(1)}, u32[]{:S(2)}, u32[]{:S(2)}) collective-permute-start(f32[80,128]{1,0:T(8,128)S(1)} %get-tuple-element.78), channel_id=1, source_target_pairs={{16,0},{32,16},{48,32},{64,48},{80,64},{96,80},{112,96},{128,112},... | collective-permute-start | bytes 122888 | tf_op jit(solution)/shard_map/ppermute | solution.py:318
  59.8 7.2 %collective-permute-start.8 = (f32[80,128]{1,0:T(8,128)S(1)}, f32[80,128]{1,0:T(8,128)S(1)}, u32[]{:S(2)}, u32[]{:S(2)}) collective-permute-start(f32[80,128]{1,0:T(8,128)S(1)} %get-tuple-element.77), channel_id=1, source_target_pairs={{0,16},{16,32},{32,48},{48,64},{64,80},{80,96},{96,112},{112,128},... | collective-permute-start | bytes 122888 | tf_op jit(solution)/shard_map/ppermute | solution.py:318
  67.0 10.5 %collective-permute-start.11 = (f32[80,128]{1,0:T(8,128)S(1)}, f32[80,128]{1,0:T(8,128)S(1)}, u32[]{:S(2)}, u32[]{:S(2)}) collective-permute-start(f32[80,128]{1,0:T(8,128)S(1)} %pad_maximum_fusion.5), channel_id=1, source_target_pairs={{1,0},{2,1},{3,2},{4,3},{5,4},{6,5},{7,6},{8,7},{9,8},{10,9},{11,1... | collective-permute-start | bytes 122888 | tf_op jit(solution)/shard_map/ppermute | solution.py:327
  72.9 4.6 %collective-permute-start.10 = (f32[80,128]{1,0:T(8,128)S(1)}, f32[80,128]{1,0:T(8,128)S(1)}, u32[]{:S(2)}, u32[]{:S(2)}) collective-permute-start(f32[80,128]{1,0:T(8,128)S(1)} %pad_maximum_fusion.4), channel_id=1, source_target_pairs={{0,1},{1,2},{2,3},{3,4},{4,5},{5,6},{6,7},{7,8},{8,9},{9,10},{10,1... | collective-permute-start | bytes 122888 | tf_op jit(solution)/shard_map/ppermute | solution.py:327
  (1 other events, 0.6 us)
where the time goes:
time: 81.1 us; the launch traced here: 80.8 us
  Pallas kernels  23.5 us (29%)
  starting transfers between devices  23.1 us (28%)
  waiting for transfers between devices  19.3 us (24%)
  local copies, waits for them, and re-layouts  12 us (15%)
  between operations  1.6 us (2%)
  other arithmetic  1.25 us (2%)
    pallas_call x11, Pallas kernels, call(): pl.pallas_call(kernel, name=name, out_shape=shapes, in_specs=in_specs, ou...  23.5 us
    ppermute x6, waiting for transfers between devices, exchange_x(): return (lax.ppermute(xu, 'gx', up), lax.ppermute(xd, 'gx', down))  18.5 us
    ppermute x6, starting transfers between devices, exchange_x(): return (lax.ppermute(xu, 'gx', up), lax.ppermute(xd, 'gx', down))  12 us
    unnamed x43, local copies, waits for them, and re-layouts  11.9 us
    ppermute x6, starting transfers between devices, exchange_y(): return (lax.ppermute(to_up, 'gy', up), lax.ppermute(to_down, 'gy', down))  11.1 us
  transfers between devices with their start and end apart: 12, of which 7 were waited for; matrix products, arithmetic and copies ran while one was open for 1% of the time, Pallas kernels for 12%

commit v1 on v0

v1 whole, which is shorter than its diff:
```python
import functools

import jax
import jax.numpy as jnp
from jax import lax
from jax.experimental import pallas as pl
from jax.experimental.pallas import tpu as pltpu
from jax.sharding import PartitionSpec as P

NR = 128
BLK = 128
SHELL = 16
STEPS = 3
PB = 8
SLOTS = PB * BLK
CX = 32
CELLS = 1024
CHUNKS = 4
CHUNK = CELLS // CHUNKS
F32 = jnp.float32
BF16 = jnp.bfloat16

OFFSETS = ((-1, -1), (-1, 0), (-1, 1), (0, -1), (0, 1), (1, -1), (1, 0), (1, 1))
NT = (((1,), (1,)), ((), ()))
NN = (((1,), (0,)), ((), ()))
VM = pl.BlockSpec(memory_space=pltpu.VMEM)
SM = pl.BlockSpec(memory_space=pltpu.SMEM)
HBM = pl.BlockSpec(memory_space=pltpu.HBM)

FACES = (slice(992, 1024), slice(0, 32), pl.ds(31, 32, stride=32), pl.ds(0, 32, stride=32))


def dot(a, b, dims=NN):
    return lax.dot_general(a, b, dims, preferred_element_type=F32)


def split2(x):
    hi = x.astype(BF16)
    return hi, (x - hi.astype(F32)).astype(BF16)


def split3(x):
    hi = x.astype(BF16)
    rest = x - hi.astype(F32)
    mid = rest.astype(BF16)
    return hi, mid, (rest - mid.astype(F32)).astype(BF16)


def flag(cond):
    return jnp.where(cond, 1.0, 0.0).astype(F32)


def neighbour(n):
    a, b = OFFSETS[n]
    x, y = lax.axis_index("gx") - a, lax.axis_index("gy") - b
    return flag((x >= 0) & (x < lax.axis_size("gx")) & (y >= 0) & (y < lax.axis_size("gy")))


def halves_of(g):
    return g[:, 0:128] + g[:, 128:256]


def pair(ref, j):
    return jnp.concatenate([ref[2 * j : 2 * j + 1, :], ref[2 * j + 1 : 2 * j + 2, :]], axis=1)


def store_pair(ref, j, row):
    ref[2 * j : 2 * j + 1, :] = row[:, 0:128]
    ref[2 * j + 1 : 2 * j + 2, :] = row[:, 128:256]


def lane_mask(cell, j):
    return lax.broadcasted_iota(jnp.int32, (128, 256), 0) == (pair(cell, j) & 127)


def pick(mask, g):
    return jnp.sum(jnp.where(mask, g[0:128, :] + g[128:256, :], 0.0), axis=0, keepdims=True)


def send_ghosts(tt, slt, xu, xd, yu, yd):
    rows = jnp.concatenate(split3(tt[...]), axis=0)
    places = ((xd, 0), (xd, 16), (xd, 32), (yd, 0), (yu, 0), (xu, 0), (xu, 16), (xu, 32))
    for j in range(4):
        g = dot(rows, slt[:, j * 256 : (j + 1) * 256])
        g = g[0:16, :] + g[16:32, :] + g[32:48, :]
        for h in range(2):
            ref, start = places[2 * j + h]
            ref[start : start + 16, :] = g[:, h * 128 : (h + 1) * 128]


def send_faces(there, theta, edge, tt, cell, coef, blocks, otf, ex, vt, xu, xd, yu, yd):
    for j in range(4):
        at = slice(j * 256, (j + 1) * 256)
        alive = jnp.concatenate(
            [jnp.full((1, 128), flag(2 * j + h < blocks), F32) for h in range(2)], axis=1
        )
        e = pair(coef, j) * (there[j] - tt[15:16, at]) * alive
        store_pair(ex, j, e)
        hi, lo = split2(jnp.where(lane_mask(cell, j), e, 0.0))
        vt[0:128, at] = hi
        vt[128:256, at] = lo
    source = halves_of(dot(otf[...], vt[...], NT))
    outs = ((xu, 48), (xd, 48), (yu, 16), (yd, 16))
    for f in range(4):
        ref, start = outs[f]
        rows = slice(f * 32, (f + 1) * 32)
        s = 1.25 * theta[FACES[f], :] - 0.5 * source[rows, :]
        ref[start : start + 32, :] = 0.125 * s - 0.25 * edge[rows, :]


def first_kernel(
    live, cell_in, coef_in, lists_in, prof_in, pops_in,
    cell, coef, prof, pops, ot, slt, otf, tt, theta, ex, vt, xu, xd, yu, yd,
    lists, gathered, edge, sems,
):
    blocks = live[0] // BLK
    copies = [
        pltpu.make_async_copy(cell_in, cell, sems.at[0]),
        pltpu.make_async_copy(lists_in, lists, sems.at[1]),
        pltpu.make_async_copy(prof_in.at[0], prof.at[0], sems.at[2]),
    ]
    for c in range(CHUNKS):
        rows = pl.ds(c * CHUNK, CHUNK)
        copies.append(pltpu.make_async_copy(pops_in.at[:, rows, :], pops.at[:, rows, :], sems.at[3 + c]))
    copies.append(pltpu.make_async_copy(coef_in, coef, sems.at[3 + CHUNKS]))
    copies.append(pltpu.make_async_copy(prof_in.at[1], prof.at[1], sems.at[4 + CHUNKS]))
    for c in copies:
        c.start()
    sub = lax.broadcasted_iota(jnp.int32, (CELLS, BLK), 0)
    f = lax.broadcasted_iota(jnp.int32, (128, BLK), 0)
    f_row = jnp.where(f < 32, f + 992, jnp.where(f < 64, f - 32, jnp.where(f < 96, f * 32 - 2017, f * 32 - 3072)))
    copies[0].wait()
    for b in range(PB):
        at = slice(b * BLK, (b + 1) * BLK)
        row = cell[b : b + 1, :] >> 7
        ot[:, at] = jnp.where(sub == row, 1.0, 0.0).astype(BF16)
        otf[:, at] = jnp.where(f_row == row, 1.0, 0.0).astype(BF16)
    copies[1].wait()
    for b in range(PB):
        at = slice(b * BLK, (b + 1) * BLK)
        slt[:, at] = jnp.where(sub == lists[b : b + 1, :], 1.0, 0.0).astype(BF16)
    copies[2].wait()
    for b in range(PB):
        at = slice(b * BLK, (b + 1) * BLK)
        tt[:, at] = prof[0, at, :].T[NR - SHELL :, :]
    send_ghosts(tt, slt, xu, xd, yu, yd)
    for c in range(CHUNKS):
        copies[3 + c].wait()
        parts = []
        for h in range(CHUNK // 128):
            at = slice(c * CHUNK + h * 128, c * CHUNK + (h + 1) * 128)
            total = pops[0, at, :]
            for i in range(1, 7):
                total = total + pops[i, at, :]
            theta[at, :] = total
            parts.append(jnp.concatenate(split2(total.T), axis=0))
        rows = jnp.concatenate(parts, axis=1)
        for j in range(4):
            at = slice(j * 256, (j + 1) * 256)
            g = dot(rows, ot[c * CHUNK : (c + 1) * CHUNK, at])
            gathered[:, at] = g if c == 0 else gathered[:, at] + g
    for i in range(4):
        edge[i * 32 : (i + 1) * 32, :] = pops[i + 1, FACES[i], :]
    copies[3 + CHUNKS].wait()
    there = [pick(lane_mask(cell, j), gathered[:, j * 256 : (j + 1) * 256]) for j in range(4)]
    send_faces(there, theta, edge, tt, cell, coef, blocks, otf, ex, vt, xu, xd, yu, yd)
    copies[4 + CHUNKS].wait()


def stream_kernel(last, has_faces, *refs):
    if has_faces:
        faces, refs = refs[0], refs[1:]
    if last:
        pops, theta, vt, ot, out, strip3, strip4, source, new, sems = refs
    else:
        pops, theta, vt, ot, cell, new, theta_new, edge, there, source, rows = refs
    for j in range(4):
        at = slice(j * 256, (j + 1) * 256)
        source[at, :] = 1.25 * theta[at, :] - 0.5 * halves_of(dot(ot[at, :], vt[...], NT))
    y = lax.broadcasted_iota(jnp.int32, (32, 128), 0)
    z = lax.broadcasted_iota(jnp.int32, (32, 128), 1)

    def row(x, _):
        at = pl.ds(pl.multiple_of(x * 32, 32), 32)
        before = pl.ds(pl.multiple_of(jnp.maximum(x - 1, 0) * 32, 32), 32)
        after = pl.ds(pl.multiple_of(jnp.minimum(x + 1, CX - 1) * 32, 32), 32)
        s = 0.125 * source[at, :]
        n0 = 2.0 * s - 0.25 * pops[0, at, :]
        new[0, at, :] = n0
        n1 = flag(x > 0) * (0.125 * source[before, :] - 0.25 * pops[1, before, :])
        new[1, at, :] = n1
        n2 = flag(x < CX - 1) * (0.125 * source[after, :] - 0.25 * pops[2, after, :])
        new[2, at, :] = n2
        n3 = jnp.where(y == 0, 0.0, pltpu.roll(s - 0.25 * pops[3, at, :], 1, 0))
        new[3, at, :] = n3
        n4 = jnp.where(y == 31, 0.0, pltpu.roll(s - 0.25 * pops[4, at, :], 31, 0))
        new[4, at, :] = n4
        n5 = jnp.where(z == 0, 0.0, pltpu.roll(s - 0.25 * pops[5, at, :], 1, 1))
        new[5, at, :] = n5
        n6 = jnp.where(z == 127, 0.0, pltpu.roll(s - 0.25 * pops[6, at, :], 127, 1))
        new[6, at, :] = n6
        if not last:
            theta_new[at, :] = ((n0 + n1) + (n2 + n3)) + ((n4 + n5) + n6)
        return 0

    def carry_faces(c):
        parts = (
            (0, 1, slice(32, 64), faces[32:64, :]),
            (CHUNKS - 1, 2, slice(960, 992), faces[0:32, :]),
            (c, 3, pl.ds(c * CHUNK + 1, 8, stride=32), faces[96 + c * 8 : 104 + c * 8, :]),
            (c, 4, pl.ds(c * CHUNK + 30, 8, stride=32), faces[64 + c * 8 : 72 + c * 8, :]),
        )
        for chunk, i, at, face in parts:
            if chunk == c:
                new[i, at, :] = new[i, at, :] - 0.25 * face
                if not last:
                    theta_new[at, :] = theta_new[at, :] - 0.25 * face

    copies = []
    for c in range(CHUNKS):
        lax.fori_loop(c * 8, (c + 1) * 8, row, 0, unroll=2)
        if has_faces:
            carry_faces(c)
        if last:
            at = pl.ds(c * CHUNK, CHUNK)
            copies.append(pltpu.make_async_copy(new.at[:, at, :], out.at[:, at, :], sems.at[c]))
            copies[-1].start()
            for x in range(c * 8, (c + 1) * 8):
                strip3[x] = new[3, x * 32 : x * 32 + 8, :]
                strip4[x] = new[4, x * 32 + 24 : x * 32 + 32, :]
    if last:
        for copy in copies:
            copy.wait()
        return
    for b in range(PB):
        at = slice(b * BLK, (b + 1) * BLK)
        hi, lo = split2(theta_new[at, :].T)
        rows[0:128, at] = hi
        rows[128:256, at] = lo
    for j in range(4):
        store_pair(there, j, pick(lane_mask(cell, j), dot(rows[...], ot[:, j * 256 : (j + 1) * 256])))
    for i in range(4):
        edge[i * 32 : (i + 1) * 32, :] = new[i + 1, FACES[i], :]


def prepare_kernel(rate, blocks, rc, halves):
    for b in range(PB):
        rc[b * BLK : (b + 1) * BLK, :] = jnp.broadcast_to(rate[b : b + 1, :], (BLK, NR)).T
        for k in range(4):
            hi, lo = split2(blocks[b, k])
            halves[b, k, :, 0:128] = hi
            halves[b, k, :, 128:256] = lo


def temp_now(b, at, blocks, prof, base, flow):
    added = jnp.concatenate([jnp.zeros((NR - SHELL, BLK), F32), flow[:, at]], axis=0).T
    alive = flag(b < blocks)
    return alive * (base[at, :] + added) + (1.0 - alive) * prof[0, at, :]


def mix_kernel(first, last, *refs):
    if first:
        live, prof, radial, rc, *refs = refs
    else:
        live, prof, radial, rc, base_in, flow, conc_in, *refs = refs
    if last:
        base, out, conc_new, sems = refs
    else:
        base, ttb, conc_new = refs
    blocks = live[0] // BLK
    wide = []
    for c in range(2):
        hi, lo = split2(radial[c])
        top = jnp.concatenate([hi, lo], axis=1)
        wide.append(jnp.concatenate([top, jnp.concatenate([hi, jnp.zeros_like(hi)], axis=1)], axis=0))
    copies = []
    for b in range(PB):
        at = slice(b * BLK, (b + 1) * BLK)
        conc = prof[1, at, :] if first else conc_in[at, :]
        temp = prof[0, at, :] if first else temp_now(b, at, blocks, prof, base_in, flow)
        alive = flag(b < blocks)
        rate = rc[at, :] * conc * jnp.exp(0.5 * jnp.tanh(temp - 1.0))
        value = halves_of(dot(jnp.concatenate(split2(temp), axis=1), wide[0])) + rate
        base[at, :] = value
        if not last:
            ttb[:, at] = value.T[NR - SHELL :, :]
        value = halves_of(dot(jnp.concatenate(split2(conc), axis=1), wide[1])) - rate
        conc_new[at, :] = alive * value + (1.0 - alive) * conc
        if last and b % 2 == 1:
            two = pl.ds((b - 1) * BLK, 2 * BLK)
            copies.append(pltpu.make_async_copy(conc_new.at[two, :], out.at[1, two, :], sems.at[b // 2]))
            copies[-1].start()
    for copy in copies:
        copy.wait()


def contact_part(blocks, cols, ex, tt, halves, rxu, rxd, ryu, ryd, extended, store):
    for b in range(PB):
        alive = flag(b < blocks)
        hi, lo = split2(tt[:, b * BLK : (b + 1) * BLK] * alive)
        extended[b, 0:16, :] = hi
        extended[b, 16:32, :] = lo
        extended[b, 32:48, :] = jnp.full((16, 128), alive, F32).astype(BF16)
    places = ((ryd, 48), (rxd, 16), (ryu, 48), (ryd, 0), (ryu, 0), (ryd, 64), (rxu, 16), (ryu, 64))
    for n in range(8):
        ref, start = places[n]
        there = neighbour(n)
        hi, lo = split2(ref[start : start + 16, :] * there)
        extended[8 + n, 0:16, :] = hi
        extended[8 + n, 16:32, :] = lo
        extended[8 + n, 32:48, :] = jnp.full((16, 128), there, F32).astype(BF16)
    row = lax.broadcasted_iota(jnp.int32, (16, 128), 0)
    for b in range(PB):
        at = slice(b * BLK, (b + 1) * BLK)
        total = None
        for k in range(4):
            x = extended[cols[k, b]]
            g = dot(jnp.concatenate([x, x], axis=1), halves[b, k], NT)
            total = g if total is None else total + g
        flow = total[0:16, :] + total[16:32, :] - total[32:33, :] * tt[:, at]
        store(b, at, jnp.where(row == 15, flow + ex[b : b + 1, :], flow))


def middle_kernel(
    live, cols, ex_in, tt_in, ttb, halves, rxu, rxd, ryu, ryd, theta_in, there_in, edge, cell, coef, otf, slt,
    flow, tt, theta, faces, ex, vt, xu, xd, yu, yd, extended,
):
    blocks = live[0] // BLK

    def store(b, at, value):
        flow[:, at] = value
        alive = flag(b < blocks)
        tt[:, at] = alive * (ttb[:, at] + value) + (1.0 - alive) * tt_in[:, at]

    contact_part(blocks, cols, ex_in, tt_in, halves, rxu, rxd, ryu, ryd, extended, store)
    send_ghosts(tt, slt, xu, xd, yu, yd)
    theta[...] = theta_in[...]
    came = ((rxd, 48, 1), (rxu, 48, 6), (ryd, 16, 3), (ryu, 16, 4))
    for f in range(4):
        ref, start, n = came[f]
        face = ref[start : start + 32, :] * neighbour(n)
        faces[f * 32 : (f + 1) * 32, :] = face
        theta[FACES[f], :] = theta[FACES[f], :] + face
    rows = jnp.concatenate(split2(faces[...].T), axis=0)
    there = []
    for j in range(4):
        more = pick(lane_mask(cell, j), dot(rows, otf[:, j * 256 : (j + 1) * 256]))
        there.append(pair(there_in, j) + more)
    send_faces(there, theta, edge, tt, cell, coef, blocks, otf, ex, vt, xu, xd, yu, yd)


def last_kernel(
    live, cols, prof, base, ex, tt, halves, rxu, rxd, ryu, ryd, strip3, strip4, prof_in, pops_in,
    profiles, pops, extended, flow, temp, face1, face2, patch3, patch4, sems,
):
    blocks = live[0] // BLK
    face1[...] = rxu[48:80, :] * neighbour(6)
    face2[...] = rxd[48:80, :] * neighbour(1)
    y = lax.broadcasted_iota(jnp.int32, (8, 128), 0)
    for x in range(CX):
        patch3[x] = jnp.where(y == 0, ryu[16 + x : 17 + x, :] * neighbour(4), strip3[x])
        patch4[x] = jnp.where(y == 7, ryd[16 + x : 17 + x, :] * neighbour(3), strip4[x])
    copies = [
        pltpu.make_async_copy(face1, pops.at[1, 0], sems.at[0]),
        pltpu.make_async_copy(face2, pops.at[2, CX - 1], sems.at[1]),
        pltpu.make_async_copy(patch3, pops.at[3, :, 0:8, :], sems.at[2]),
        pltpu.make_async_copy(patch4, pops.at[4, :, 24:32, :], sems.at[3]),
    ]
    for c in copies:
        c.start()

    def store(b, at, value):
        flow[:, at] = value
        temp[at, :] = temp_now(b, at, blocks, prof, base, flow)
        if b % 2 == 1:
            two = pl.ds((b - 1) * BLK, 2 * BLK)
            copies.append(pltpu.make_async_copy(temp.at[two, :], profiles.at[0, two, :], sems.at[4 + b // 2]))
            copies[-1].start()

    contact_part(blocks, cols, ex, tt, halves, rxu, rxd, ryu, ryd, extended, store)
    for c in copies:
        c.wait()


def call(kernel, name, ins, in_specs, outs, out_specs=None, scratch=(), us=2, aliases=None, mib=8):
    shapes = [jax.ShapeDtypeStruct(s, d) for s, d in outs]
    return pl.pallas_call(
        kernel,
        name=name,
        out_shape=shapes,
        in_specs=in_specs,
        out_specs=[VM] * len(outs) if out_specs is None else out_specs,
        scratch_shapes=list(scratch),
        compiler_params=pltpu.CompilerParams(vmem_limit_bytes=mib * 1024 * 1024),
        input_output_aliases=aliases or {},
        cost_estimate=pl.CostEstimate(flops=us * 10**8, bytes_accessed=us * 3 * 10**6, transcendentals=0),
    )(*ins)


def exchange(axis, to_up, to_down):
    n = lax.axis_size(axis)
    up = [(i, (i + 1) % n) for i in range(n)]
    down = [(j, i) for i, j in up]
    return lax.ppermute(to_up, axis, up), lax.ppermute(to_down, axis, down)


def on_device(
    profiles, radial, rate_const, transfer_coef, live_count, send_lists, cell_index, contact_cols, contact_blocks, populations
):
    blocks = contact_blocks.reshape(PB, 4, BLK, BLK)
    rate = rate_const.reshape(PB, BLK)
    cols = contact_cols.T
    plane, lanes, shells, square = ((SLOTS, 128), F32), ((PB, BLK), F32), ((SHELL, SLOTS), F32), ((128, 128), F32)
    lattice = ((7, CELLS, 128), F32)
    wide = ((256, 1024), BF16)
    sends = [((80, 128), F32)] * 2 + [((48, 128), F32)] * 2
    ext_s = pltpu.VMEM((16, 48, 128), BF16)

    stay = [
        pltpu.with_memory_space_constraint(a, pltpu.HBM)
        for a in (
            cell_index.reshape(PB, BLK),
            transfer_coef.reshape(PB, BLK),
            send_lists,
            profiles,
            populations.reshape(7, CELLS, 128),
        )
    ]
    cell, coef, prof, pops, ot, slt, otf, tt, theta, ex, vt, xu, xd, yu, yd = call(
        first_kernel, "first", (live_count, *stay),
        [SM] + [HBM] * 5,
        [((PB, BLK), jnp.int32), lanes, ((2, SLOTS, NR), F32), lattice, ((CELLS, SLOTS), BF16), ((SLOTS, SLOTS), BF16),
         ((128, SLOTS), BF16), shells, plane, lanes, wide] + sends,
        scratch=[pltpu.VMEM((PB, BLK), jnp.int32), pltpu.VMEM((256, 1024), F32), pltpu.VMEM((128, 128), F32),
                 pltpu.SemaphoreType.DMA((5 + CHUNKS,))],
        us=6,
    )
    faces = base = flow = conc = there = edge = None
    for step in range(STEPS):
        final = step == STEPS - 1
        rxu, rxd = exchange("gx", xu, xd)
        inputs = (() if step == 0 else (faces,)) + (pops, theta, vt, ot) + (() if final else (cell,))
        if final:
            outs, specs = [lattice] + [((CX, 8, 128), F32)] * 2, [HBM, VM, VM]
            scratch = [pltpu.VMEM(*plane), pltpu.VMEM(*lattice), pltpu.SemaphoreType.DMA((CHUNKS,))]
        else:
            outs, specs = [lattice, plane, square, lanes], None
            scratch = [pltpu.VMEM(*plane), pltpu.VMEM(*wide)]
        streamed = call(
            functools.partial(stream_kernel, final, step > 0), "stream",
            inputs, [VM] * len(inputs), outs, out_specs=specs, scratch=scratch, us=4,
        )
        rxu, rxd, streamed = lax.optimization_barrier((rxu, rxd, streamed))
        ryu, ryd = exchange(
            "gy",
            jnp.concatenate([yu, rxd[32:48], rxu[32:48]], axis=0),
            jnp.concatenate([yd, rxd[0:16], rxu[0:16]], axis=0),
        )
        received = (rxu, rxd, ryu, ryd)
        if step == 0:
            rc, halves = call(
                prepare_kernel, "prepare", (rate, blocks), [VM, VM], [plane, ((PB, 4, BLK, 256), BF16)], us=1
            )
        inputs = (live_count, prof, radial, rc) + (() if step == 0 else (base, flow, conc))
        if final:
            outs, specs = [plane, ((2, SLOTS, NR), F32)], [VM, HBM]
            scratch = [pltpu.VMEM(*plane), pltpu.SemaphoreType.DMA((4,))]
        else:
            outs, specs, scratch = [plane, shells, plane], None, []
        mixed = call(
            functools.partial(mix_kernel, step == 0, final), "mix",
            inputs, [SM] + [VM] * (len(inputs) - 1), outs, out_specs=specs, scratch=scratch, us=1,
        )
        if final:
            return call(
                last_kernel, "last",
                (live_count, cols, prof, mixed[0], ex, tt, halves, *received, *streamed[1:],
                 mixed[1], streamed[0].reshape(7, CX, 32, 128)),
                [SM] * 2 + [VM] * 11 + [HBM] * 2,
                [((2, SLOTS, NR), F32), ((7, CX, 32, 128), F32)],
                out_specs=[HBM, HBM],
                scratch=[ext_s, pltpu.VMEM(*shells), pltpu.VMEM(*plane)] + [pltpu.VMEM((32, 128), F32)] * 2
                + [pltpu.VMEM((CX, 8, 128), F32)] * 2 + [pltpu.SemaphoreType.DMA((8,))],
                aliases={13: 0, 14: 1},
            )
        base, ttb, conc = mixed
        pops, theta, edge, there = streamed
        flow, tt, theta, faces, ex, vt, xu, xd, yu, yd = call(
            middle_kernel, "middle",
            (live_count, cols, ex, tt, ttb, halves, *received, theta, there, edge, cell, coef, otf, slt),
            [SM] * 2 + [VM] * 15,
            [shells, shells, plane, square, lanes, wide] + sends,
            scratch=[ext_s],
        )


def solution(mesh):
    return jax.shard_map(
        on_device,
        mesh=mesh,
        in_specs=(
            P(None, ("gx", "gy"), None),
            P(),
            P(("gx", "gy")),
            P(("gx", "gy")),
            P(("gx", "gy")),
            P(("gx", "gy"), None),
            P(("gx", "gy")),
            P(("gx", "gy"), None),
            P(("gx", "gy"), None, None, None),
            P(None, "gx", "gy", None),
        ),
        out_specs=(P(None, ("gx", "gy"), None), P(None, "gx", "gy", None)),
        check_vma=False,
    )
```

time: 81.1 us -> 61.3 us (0.76)
  the two profiles are of different devices: /device:TPU:1 before, /device:TPU:70 now
where the time goes in v1:
time: 61.3 us; the launch traced here: 61.1 us
  Pallas kernels  23.3 us (38%)
  starting transfers between devices  20.4 us (33%)
  waiting for transfers between devices  15.7 us (26%)
  between operations  1.63 us (3%)
    pallas_call x11, Pallas kernels, call(): pl.pallas_call(kernel, name=name, out_shape=shapes, in_specs=in_specs, ou...  23.3 us
    ppermute x12, starting transfers between devices, exchange(): return (lax.ppermute(to_up, axis, up), lax.ppermute(to_down, axis, down))  20.4 us
    ppermute x12, waiting for transfers between devices, exchange(): return (lax.ppermute(to_up, axis, up), lax.ppermute(to_down, axis, down))  15.7 us
  transfers between devices with their start and end apart: 12, of which 7 were waited for; matrix products, arithmetic and copies ran while one was open for 0% of the time, Pallas kernels for 20%

profile of v1, /device:TPU:70, one launch (start us, length us, event | category | flops | bytes accessed | tf_op | source)
XLA Modules:
  0.0 61.1 jit_solution(10512038281923880475)
XLA Ops:
  1.3 4.1 %first.1 = (s32[8,128]{1,0:T(8,128)S(1)}, f32[8,128]{1,0:T(8,128)S(1)}, f32[2,1024,128]{2,1,0:T(8,128)S(1)}, f32[7,1024,128]{2,1,0:T(8,128)S(1)}, bf16[1024,1024...) custom-call(s32[1]{0:T(128)S(6)} %copy.16.live.refs_0_, ...), custom_call_target="tpu_custom_call" | custom-call | flops 600000000 | bytes 18000000 | tf_op jit(solution)/shard_map/first/pallas_call | solution.py:387
  5.4 0.0 copy-start
  5.4 0.0 copy-start.3
  5.4 4.5 %collective-permute-start = (f32[80,128]{1,0:T(8,128)S(1)}, f32[80,128]{1,0:T(8,128)S(1)}, u32[]{:S(2)}, u32[]{:S(2)}) collective-permute-start(f32[80,128]{1,0:T(8,128)S(1)} %get-tuple-element.82), channel_id=1, source_target_pairs={{0,16},{16,32},{32,48},{48,64},{64,80},{80,96},{96,112},{112,128},... | collective-permute-start | bytes 122888 | tf_op jit(solution)/shard_map/ppermute | solution.py:404
  9.9 3.0 %stream.3 = (f32[7,1024,128]{2,1,0:T(8,128)S(1)}, f32[1024,128]{1,0:T(8,128)S(1)}, f32[128,128]{1,0:T(8,128)S(1)}, f32[8,128]{1,0:T(8,128)S(1)}) custom-call(f32[7,1024,128]{2,1,0:T(8,128)S(1)} %get-tuple-element.84.refs_0_, f32[1024,128]{1,0:T(8,128)S(1)} %get-tuple-element.85.refs_1_, bf16[256,1024]{1,0:T(8,128)(2,1)S(1)} %get-tuple-element.86.refs_2_, ...), custom_call_target="tpu_custom_call" | custom-call | flops 400000000 | bytes 12000000 | tf_op jit(solution)/shard_map/stream/pallas_call | solution.py:387
  12.8 0.0 copy-start.2
  12.9 5.3 %collective-permute-done.1.rxd = f32[80,128]{1,0:T(8,128)S(1)} collective-permute-done((f32[80,128]{1,0:T(8,128)S(1)}, f32[80,128]{1,0:T(8,128)S(1)}, u32[]{:S(2)}, u32[]{:S(2)}) %collective-permute-start.1) | collective-permute-done | bytes 40992 | tf_op jit(solution)/shard_map/ppermute | solution.py:404
  18.2 0.1 collective-permute-start.2
  18.3 3.8 %collective-permute-start.3 = (f32[80,128]{1,0:T(8,128)S(1)}, f32[80,128]{1,0:T(8,128)S(1)}, u32[]{:S(2)}, u32[]{:S(2)}) collective-permute-start(f32[80,128]{1,0:T(8,128)S(1)} %pad_maximum_fusion.1), channel_id=1, source_target_pairs={{1,0},{2,1},{3,2},{4,3},{5,4},{6,5},{7,6},{8,7},{9,8},{10,9},{11,1... | collective-permute-start | bytes 122888 | tf_op jit(solution)/shard_map/ppermute | solution.py:404
  22.1 0.5 prepare.1
  22.6 0.5 mix.3
  23.2 0.6 %collective-permute-done.2.ryu = f32[80,128]{1,0:T(8,128)S(1)} collective-permute-done((f32[80,128]{1,0:T(8,128)S(1)}, f32[80,128]{1,0:T(8,128)S(1)}, u32[]{:S(2)}, u32[]{:S(2)}) %collective-permute-start.2) | collective-permute-done | bytes 40992 | tf_op jit(solution)/shard_map/ppermute | solution.py:404
  23.8 0.3 collective-permute-done.3.ryd
  24.1 2.4 %middle.2 = (f32[16,1024]{1,0:T(8,128)S(1)}, f32[16,1024]{1,0:T(8,128)S(1)}, f32[1024,128]{1,0:T(8,128)S(1)}, f32[128,128]{1,0:T(8,128)S(1)}, f32[8,128]{1,0:T(8...) custom-call(s32[1]{0:T(128)S(6)} %copy.16.live.refs_0_, ...), custom_call_target="tpu_custom_call" | custom-call | flops 200000000 | bytes 6000000 | tf_op jit(solution)/shard_map/middle/pallas_call | solution.py:387
  26.5 0.7 %collective-permute-start.4 = (f32[80,128]{1,0:T(8,128)S(1)}, f32[80,128]{1,0:T(8,128)S(1)}, u32[]{:S(2)}, u32[]{:S(2)}) collective-permute-start(f32[80,128]{1,0:T(8,128)S(1)} %get-tuple-element.109), channel_id=1, source_target_pairs={{0,16},{16,32},{32,48},{48,64},{64,80},{80,96},{96,112},{112,128},... | collective-permute-start | bytes 122888 | tf_op jit(solution)/shard_map/ppermute | solution.py:404
  27.2 1.4 %collective-permute-start.5 = (f32[80,128]{1,0:T(8,128)S(1)}, f32[80,128]{1,0:T(8,128)S(1)}, u32[]{:S(2)}, u32[]{:S(2)}) collective-permute-start(f32[80,128]{1,0:T(8,128)S(1)} %get-tuple-element.110), channel_id=1, source_target_pairs={{16,0},{32,16},{48,32},{64,48},{80,64},{96,80},{112,96},{128,112},... | collective-permute-start | bytes 122888 | tf_op jit(solution)/shard_map/ppermute | solution.py:404
  28.6 3.0 %stream.4 = (f32[7,1024,128]{2,1,0:T(8,128)S(1)}, f32[1024,128]{1,0:T(8,128)S(1)}, f32[128,128]{1,0:T(8,128)S(1)}, f32[8,128]{1,0:T(8,128)S(1)}) custom-call(f32[128,128]{1,0:T(8,128)S(1)} %get-tuple-element.111.refs_0_, f32[7,1024,128]{2,1,0:T(8,128)S(1)} %get-tuple-element.112.refs_1_, f32[1024,128]{1,0:T(8,128)S(1)} %get-tuple-element.113.refs_2_, ...), custom_call_target="tpu_custom_call" | custom-call | flops 400000000 | bytes 12000000 | tf_op jit(solution)/shard_map/stream/pallas_call | solution.py:387
  31.7 4.2 %collective-permute-done.5.rxd = f32[80,128]{1,0:T(8,128)S(1)} collective-permute-done((f32[80,128]{1,0:T(8,128)S(1)}, f32[80,128]{1,0:T(8,128)S(1)}, u32[]{:S(2)}, u32[]{:S(2)}) %collective-permute-start.5) | collective-permute-done | bytes 40992 | tf_op jit(solution)/shard_map/ppermute | solution.py:404
  35.9 0.1 collective-permute-start.6
  36.0 3.8 %collective-permute-start.7 = (f32[80,128]{1,0:T(8,128)S(1)}, f32[80,128]{1,0:T(8,128)S(1)}, u32[]{:S(2)}, u32[]{:S(2)}) collective-permute-start(f32[80,128]{1,0:T(8,128)S(1)} %pad_maximum_fusion.3), channel_id=1, source_target_pairs={{1,0},{2,1},{3,2},{4,3},{5,4},{6,5},{7,6},{8,7},{9,8},{10,9},{11,1... | collective-permute-start | bytes 122888 | tf_op jit(solution)/shard_map/ppermute | solution.py:404
  39.8 0.6 mix.4
  40.5 1.1 %collective-permute-done.6.ryu = f32[80,128]{1,0:T(8,128)S(1)} collective-permute-done((f32[80,128]{1,0:T(8,128)S(1)}, f32[80,128]{1,0:T(8,128)S(1)}, u32[]{:S(2)}, u32[]{:S(2)}) %collective-permute-start.6) | collective-permute-done | bytes 40992 | tf_op jit(solution)/shard_map/ppermute | solution.py:404
  41.5 2.4 %middle.3 = (f32[16,1024]{1,0:T(8,128)S(1)}, f32[16,1024]{1,0:T(8,128)S(1)}, f32[1024,128]{1,0:T(8,128)S(1)}, f32[128,128]{1,0:T(8,128)S(1)}, f32[8,128]{1,0:T(8...) custom-call(s32[1]{0:T(128)S(6)} %copy.16.live.refs_0_, ...), custom_call_target="tpu_custom_call" | custom-call | flops 200000000 | bytes 6000000 | tf_op jit(solution)/shard_map/middle/pallas_call | solution.py:387
  43.9 1.0 %collective-permute-start.8 = (f32[80,128]{1,0:T(8,128)S(1)}, f32[80,128]{1,0:T(8,128)S(1)}, u32[]{:S(2)}, u32[]{:S(2)}) collective-permute-start(f32[80,128]{1,0:T(8,128)S(1)} %get-tuple-element.131), channel_id=1, source_target_pairs={{0,16},{16,32},{32,48},{48,64},{64,80},{80,96},{96,112},{112,128},... | collective-permute-start | bytes 122888 | tf_op jit(solution)/shard_map/ppermute | solution.py:404
  44.9 1.1 %collective-permute-start.9 = (f32[80,128]{1,0:T(8,128)S(1)}, f32[80,128]{1,0:T(8,128)S(1)}, u32[]{:S(2)}, u32[]{:S(2)}) collective-permute-start(f32[80,128]{1,0:T(8,128)S(1)} %get-tuple-element.132), channel_id=1, source_target_pairs={{16,0},{32,16},{48,32},{64,48},{80,64},{96,80},{112,96},{128,112},... | collective-permute-start | bytes 122888 | tf_op jit(solution)/shard_map/ppermute | solution.py:404
  46.0 3.4 %stream.5 = (f32[7,1024,128]{2,1,0:T(8,128)}, f32[32,8,128]{2,1,0:T(8,128)S(1)}, f32[32,8,128]{2,1,0:T(8,128)S(1)}) custom-call(f32[128,128]{1,0:T(8,128)S(1)} %get-tuple-element.133.refs_0_, f32[7,1024,128]{2,1,0:T(8,128)S(1)} %get-tuple-element.134.refs_1_, f32[1024,128]{1,0:T(8,128)S(1)} %get-tuple-element.135.refs_2_, ...), custom_call_target="tpu_custom_call" | custom-call | flops 400000000 | bytes 12000000 | tf_op jit(solution)/shard_map/stream/pallas_call | solution.py:387
  49.4 3.7 %collective-permute-done.9.rxd = f32[80,128]{1,0:T(8,128)S(1)} collective-permute-done((f32[80,128]{1,0:T(8,128)S(1)}, f32[80,128]{1,0:T(8,128)S(1)}, u32[]{:S(2)}, u32[]{:S(2)}) %collective-permute-start.9) | collective-permute-done | bytes 40992 | tf_op jit(solution)/shard_map/ppermute | solution.py:404
  53.1 0.1 collective-permute-start.10
  53.2 3.8 %collective-permute-start.11 = (f32[80,128]{1,0:T(8,128)S(1)}, f32[80,128]{1,0:T(8,128)S(1)}, u32[]{:S(2)}, u32[]{:S(2)}) collective-permute-start(f32[80,128]{1,0:T(8,128)S(1)} %pad_maximum_fusion.5), channel_id=1, source_target_pairs={{1,0},{2,1},{3,2},{4,3},{5,4},{6,5},{7,6},{8,7},{9,8},{10,9},{11,1... | collective-permute-start | bytes 122888 | tf_op jit(solution)/shard_map/ppermute | solution.py:404
  57.1 1.2 %mix.5 = (f32[1024,128]{1,0:T(8,128)S(1)}, f32[2,1024,128]{2,1,0:T(8,128)}) custom-call(s32[1]{0:T(128)S(6)} %copy.16.live.refs_0_, f32[2,1024,128]{2,1,0:T(8,128)S(1)} %get-tuple-element.75.refs_1_.prof, f32[2,128,128]{2,1,0:T(8,128)S(1)} %copy-done.1, f32[1024,128]{1,0:T(8,128)S(1)} %get-tuple-element.76.refs_3_, ...), custom_call_target="tpu_custom_call" | custom-call | flops 100000000 | bytes 3000000 | tf_op jit(solution)/shard_map/mix/pallas_call | solution.py:387
  58.3 0.4 collective-permute-done.10.ryu
  58.8 2.2 %last.1 = (f32[2,1024,128]{2,1,0:T(8,128)}, f32[7,32,32,128]{3,2,1,0:T(8,128)}) custom-call(s32[1]{0:T(128)S(6)} %copy.16.live.refs_0_, s32[4,8]{1,0:T(4,128)S(1)} %bitcast.8, f32[2,1024,128]{2,1,0:T(8,128)S(1)} %get-tuple-element.75.refs_1_.prof, f32[1024,128]{1,0:T(8,128)S(1)} %get-tuple-element.128.base, ...), custom_call_target="tpu_custom_call", output_to_operand_aliasing={{0}: (13, {}), {1}: (14, {})} | custom-call | flops 200000000 | bytes 6000000 | tf_op jit(solution)/shard_map/last/pallas_call | solution.py:387
  (22 shorter events, 0.1 us)
Async XLA Ops:
  5.4 16.8 %copy-start = (f32[8,4,128,128]{3,2,1,0:T(8,128)S(1)}, f32[8,4,128,128]{3,2,1,0:T(8,128)}, u32[]{:S(2)}) copy-start(f32[8,4,128,128]{3,2,1,0:T(8,128)} %blocks.1) | copy-start | bytes 6291460
  5.4 16.8 %copy-start.3 = (f32[1024]{0:T(1024)S(1)}, f32[1024]{0:T(1024)}, u32[]{:S(2)}) copy-start(f32[1024]{0:T(1024)} %param.12) | copy-start | bytes 12292
  5.4 7.5 %collective-permute-start = (f32[80,128]{1,0:T(8,128)S(1)}, f32[80,128]{1,0:T(8,128)S(1)}, u32[]{:S(2)}, u32[]{:S(2)}) collective-permute-start(f32[80,128]{1,0:T(8,128)S(1)} %get-tuple-element.82), channel_id=1, source_target_pairs={{0,16},{16,32},{32,48},{48,64},{64,80},{80,96},{96,112},{112,128},... | collective-permute-start | bytes 122888 | tf_op jit(solution)/shard_map/ppermute | solution.py:404
  9.9 8.3 %collective-permute-start.1 = (f32[80,128]{1,0:T(8,128)S(1)}, f32[80,128]{1,0:T(8,128)S(1)}, u32[]{:S(2)}, u32[]{:S(2)}) collective-permute-start(f32[80,128]{1,0:T(8,128)S(1)} %get-tuple-element.83), channel_id=1, source_target_pairs={{16,0},{32,16},{48,32},{64,48},{80,64},{96,80},{112,96},{128,112},... | collective-permute-start | bytes 122888 | tf_op jit(solution)/shard_map/ppermute | solution.py:404
  9.9 12.8 %copy-start.1 = (f32[2,128,128]{2,1,0:T(8,128)S(1)}, f32[2,128,128]{2,1,0:T(8,128)}, u32[]{:S(2)}) copy-start(f32[2,128,128]{2,1,0:T(8,128)} %refs_2_.5) | copy-start | bytes 393220
  12.8 11.3 %copy-start.2 = (s32[8,4]{0,1:T(4,128)S(1)}, s32[8,4]{0,1:T(4,128)}, u32[]{:S(2)}) copy-start(s32[8,4]{0,1:T(4,128)} %param.17) | copy-start | bytes 388
  18.2 5.6 %collective-permute-start.2 = (f32[80,128]{1,0:T(8,128)S(1)}, f32[80,128]{1,0:T(8,128)S(1)}, u32[]{:S(2)}, u32[]{:S(2)}) collective-permute-start(f32[80,128]{1,0:T(8,128)S(1)} %pad_maximum_fusion), channel_id=1, source_target_pairs={{0,1},{1,2},{2,3},{3,4},{4,5},{5,6},{6,7},{7,8},{8,9},{9,10},{10,1... | collective-permute-start | bytes 122888 | tf_op jit(solution)/shard_map/ppermute | solution.py:404
  18.3 5.8 %collective-permute-start.3 = (f32[80,128]{1,0:T(8,128)S(1)}, f32[80,128]{1,0:T(8,128)S(1)}, u32[]{:S(2)}, u32[]{:S(2)}) collective-permute-start(f32[80,128]{1,0:T(8,128)S(1)} %pad_maximum_fusion.1), channel_id=1, source_target_pairs={{1,0},{2,1},{3,2},{4,3},{5,4},{6,5},{7,6},{8,7},{9,8},{10,9},{11,1... | collective-permute-start | bytes 122888 | tf_op jit(solution)/shard_map/ppermute | solution.py:404
  26.5 5.2 %collective-permute-start.4 = (f32[80,128]{1,0:T(8,128)S(1)}, f32[80,128]{1,0:T(8,128)S(1)}, u32[]{:S(2)}, u32[]{:S(2)}) collective-permute-start(f32[80,128]{1,0:T(8,128)S(1)} %get-tuple-element.109), channel_id=1, source_target_pairs={{0,16},{16,32},{32,48},{48,64},{64,80},{80,96},{96,112},{112,128},... | collective-permute-start | bytes 122888 | tf_op jit(solution)/shard_map/ppermute | solution.py:404
  27.2 8.7 %collective-permute-start.5 = (f32[80,128]{1,0:T(8,128)S(1)}, f32[80,128]{1,0:T(8,128)S(1)}, u32[]{:S(2)}, u32[]{:S(2)}) collective-permute-start(f32[80,128]{1,0:T(8,128)S(1)} %get-tuple-element.110), channel_id=1, source_target_pairs={{16,0},{32,16},{48,32},{64,48},{80,64},{96,80},{112,96},{128,112},... | collective-permute-start | bytes 122888 | tf_op jit(solution)/shard_map/ppermute | solution.py:404
  35.9 5.6 %collective-permute-start.6 = (f32[80,128]{1,0:T(8,128)S(1)}, f32[80,128]{1,0:T(8,128)S(1)}, u32[]{:S(2)}, u32[]{:S(2)}) collective-permute-start(f32[80,128]{1,0:T(8,128)S(1)} %pad_maximum_fusion.2), channel_id=1, source_target_pairs={{0,1},{1,2},{2,3},{3,4},{4,5},{5,6},{6,7},{7,8},{8,9},{9,10},{10,1... | collective-permute-start | bytes 122888 | tf_op jit(solution)/shard_map/ppermute | solution.py:404
  36.0 5.5 %collective-permute-start.7 = (f32[80,128]{1,0:T(8,128)S(1)}, f32[80,128]{1,0:T(8,128)S(1)}, u32[]{:S(2)}, u32[]{:S(2)}) collective-permute-start(f32[80,128]{1,0:T(8,128)S(1)} %pad_maximum_fusion.3), channel_id=1, source_target_pairs={{1,0},{2,1},{3,2},{4,3},{5,4},{6,5},{7,6},{8,7},{9,8},{10,9},{11,1... | collective-permute-start | bytes 122888 | tf_op jit(solution)/shard_map/ppermute | solution.py:404
  43.9 5.5 %collective-permute-start.8 = (f32[80,128]{1,0:T(8,128)S(1)}, f32[80,128]{1,0:T(8,128)S(1)}, u32[]{:S(2)}, u32[]{:S(2)}) collective-permute-start(f32[80,128]{1,0:T(8,128)S(1)} %get-tuple-element.131), channel_id=1, source_target_pairs={{0,16},{16,32},{32,48},{48,64},{64,80},{80,96},{96,112},{112,128},... | collective-permute-start | bytes 122888 | tf_op jit(solution)/shard_map/ppermute | solution.py:404
  44.9 8.2 %collective-permute-start.9 = (f32[80,128]{1,0:T(8,128)S(1)}, f32[80,128]{1,0:T(8,128)S(1)}, u32[]{:S(2)}, u32[]{:S(2)}) collective-permute-start(f32[80,128]{1,0:T(8,128)S(1)} %get-tuple-element.132), channel_id=1, source_target_pairs={{16,0},{32,16},{48,32},{64,48},{80,64},{96,80},{112,96},{128,112},... | collective-permute-start | bytes 122888 | tf_op jit(solution)/shard_map/ppermute | solution.py:404
  53.1 5.6 %collective-permute-start.10 = (f32[80,128]{1,0:T(8,128)S(1)}, f32[80,128]{1,0:T(8,128)S(1)}, u32[]{:S(2)}, u32[]{:S(2)}) collective-permute-start(f32[80,128]{1,0:T(8,128)S(1)} %pad_maximum_fusion.4), channel_id=1, source_target_pairs={{0,1},{1,2},{2,3},{3,4},{4,5},{5,6},{6,7},{7,8},{8,9},{9,10},{10,1... | collective-permute-start | bytes 122888 | tf_op jit(solution)/shard_map/ppermute | solution.py:404
  53.2 5.5 %collective-permute-start.11 = (f32[80,128]{1,0:T(8,128)S(1)}, f32[80,128]{1,0:T(8,128)S(1)}, u32[]{:S(2)}, u32[]{:S(2)}) collective-permute-start(f32[80,128]{1,0:T(8,128)S(1)} %pad_maximum_fusion.5), channel_id=1, source_target_pairs={{1,0},{2,1},{3,2},{4,3},{5,4},{6,5},{7,6},{8,7},{9,8},{10,9},{11,1... | collective-permute-start | bytes 122888 | tf_op jit(solution)/shard_map/ppermute | solution.py:404

commit v2 on v1

--- a/solution.py
+++ b/solution.py
@@ -74,18 +74,22 @@
 
 
 def pick(mask, g):
-    return jnp.sum(jnp.where(mask, g[0:128, :] + g[128:256, :], 0.0), axis=0, keepdims=True)
-
-
-def send_ghosts(tt, slt, xu, xd, yu, yd):
-    rows = jnp.concatenate(split3(tt[...]), axis=0)
+    return jnp.sum(jnp.where(mask, g, 0.0), axis=0, keepdims=True)
+
+
+def send_ghosts(tt, lists, xu, xd, yu, yd):
     places = ((xd, 0), (xd, 16), (xd, 32), (yd, 0), (yu, 0), (xu, 0), (xu, 16), (xu, 32))
-    for j in range(4):
-        g = dot(rows, slt[:, j * 256 : (j + 1) * 256])
-        g = g[0:16, :] + g[16:32, :] + g[32:48, :]
-        for h in range(2):
-            ref, start = places[2 * j + h]
-            ref[start : start + 16, :] = g[:, h * 128 : (h + 1) * 128]
+    for n in range(8):
+        listed = jnp.broadcast_to(lists[n : n + 1, :], (8, BLK))
+        lane, block = listed & 127, listed >> 7
+        ref, start = places[n]
+        for h in (0, 8):
+            total = None
+            for b in range(PB):
+                shell = tt[h : h + 8, b * BLK : (b + 1) * BLK]
+                g = jnp.take_along_axis(shell, lane, axis=1, mode="promise_in_bounds")
+                total = g if b == 0 else jnp.where(block == b, g, total)
+            ref[start + h : start + h + 8, :] = total
 
 
 def send_faces(there, theta, edge, tt, cell, coef, blocks, otf, ex, vt, xu, xd, yu, yd):
@@ -99,7 +103,7 @@
         hi, lo = split2(jnp.where(lane_mask(cell, j), e, 0.0))
         vt[0:128, at] = hi
         vt[128:256, at] = lo
-    source = halves_of(dot(otf[...], vt[...], NT))
+    source = halves_of(dot(otf[0:128, :], vt[...], NT))
     outs = ((xu, 48), (xd, 48), (yu, 16), (yd, 16))
     for f in range(4):
         ref, start = outs[f]
@@ -110,8 +114,8 @@
 
 def first_kernel(
     live, cell_in, coef_in, lists_in, prof_in, pops_in,
-    cell, coef, prof, pops, ot, slt, otf, tt, theta, ex, vt, xu, xd, yu, yd,
-    lists, gathered, edge, sems,
+    cell, coef, lists, prof, pops, ot, otf, tt, theta, ex, vt, xu, xd, yu, yd,
+    gathered, edge, sems,
 ):
     blocks = live[0] // BLK
     copies = [
@@ -134,16 +138,15 @@
         at = slice(b * BLK, (b + 1) * BLK)
         row = cell[b : b + 1, :] >> 7
         ot[:, at] = jnp.where(sub == row, 1.0, 0.0).astype(BF16)
-        otf[:, at] = jnp.where(f_row == row, 1.0, 0.0).astype(BF16)
+        face = jnp.where(f_row == row, 1.0, 0.0).astype(BF16)
+        otf[0:128, at] = face
+        otf[128:256, at] = face
     copies[1].wait()
-    for b in range(PB):
-        at = slice(b * BLK, (b + 1) * BLK)
-        slt[:, at] = jnp.where(sub == lists[b : b + 1, :], 1.0, 0.0).astype(BF16)
     copies[2].wait()
     for b in range(PB):
         at = slice(b * BLK, (b + 1) * BLK)
         tt[:, at] = prof[0, at, :].T[NR - SHELL :, :]
-    send_ghosts(tt, slt, xu, xd, yu, yd)
+    send_ghosts(tt, lists, xu, xd, yu, yd)
     for c in range(CHUNKS):
         copies[3 + c].wait()
         parts = []
@@ -162,7 +165,10 @@
     for i in range(4):
         edge[i * 32 : (i + 1) * 32, :] = pops[i + 1, FACES[i], :]
     copies[3 + CHUNKS].wait()
-    there = [pick(lane_mask(cell, j), gathered[:, j * 256 : (j + 1) * 256]) for j in range(4)]
+    there = []
+    for j in range(4):
+        at = slice(j * 256, (j + 1) * 256)
+        there.append(pick(lane_mask(cell, j), gathered[0:128, at] + gathered[128:256, at]))
     send_faces(there, theta, edge, tt, cell, coef, blocks, otf, ex, vt, xu, xd, yu, yd)
     copies[4 + CHUNKS].wait()
 
@@ -173,7 +179,7 @@
     if last:
         pops, theta, vt, ot, out, strip3, strip4, source, new, sems = refs
     else:
-        pops, theta, vt, ot, cell, new, theta_new, edge, there, source, rows = refs
+        pops, theta, vt, ot, new, theta_new, edge, source = refs
     for j in range(4):
         at = slice(j * 256, (j + 1) * 256)
         source[at, :] = 1.25 * theta[at, :] - 0.5 * halves_of(dot(ot[at, :], vt[...], NT))
@@ -232,24 +238,28 @@
         for copy in copies:
             copy.wait()
         return
+    for i in range(4):
+        edge[i * 32 : (i + 1) * 32, :] = new[i + 1, FACES[i], :]
+
+
+def gather_kernel(theta, ot, cell, there, rows):
     for b in range(PB):
         at = slice(b * BLK, (b + 1) * BLK)
-        hi, lo = split2(theta_new[at, :].T)
+        hi, lo = split2(theta[at, :].T)
         rows[0:128, at] = hi
         rows[128:256, at] = lo
     for j in range(4):
-        store_pair(there, j, pick(lane_mask(cell, j), dot(rows[...], ot[:, j * 256 : (j + 1) * 256])))
-    for i in range(4):
-        edge[i * 32 : (i + 1) * 32, :] = new[i + 1, FACES[i], :]
+        g = dot(rows[...], ot[:, j * 256 : (j + 1) * 256])
+        store_pair(there, j, pick(lane_mask(cell, j), g[0:128, :] + g[128:256, :]))
 
 
 def prepare_kernel(rate, blocks, rc, halves):
     for b in range(PB):
         rc[b * BLK : (b + 1) * BLK, :] = jnp.broadcast_to(rate[b : b + 1, :], (BLK, NR)).T
         for k in range(4):
-            hi, lo = split2(blocks[b, k])
-            halves[b, k, :, 0:128] = hi
-            halves[b, k, :, 128:256] = lo
+            hi, lo = split2(blocks[b, k].T)
+            halves[b, k * 256 : k * 256 + 128, :] = hi
+            halves[b, k * 256 + 128 : k * 256 + 256, :] = lo
 
 
 def temp_now(b, at, blocks, prof, base, flow):
@@ -294,7 +304,7 @@
         copy.wait()
 
 
-def contact_part(blocks, cols, ex, tt, halves, rxu, rxd, ryu, ryd, extended, store):
+def extend(blocks, tt, rxu, rxd, ryu, ryd, extended):
     for b in range(PB):
         alive = flag(b < blocks)
         hi, lo = split2(tt[:, b * BLK : (b + 1) * BLK] * alive)
@@ -309,31 +319,26 @@
         extended[8 + n, 0:16, :] = hi
         extended[8 + n, 16:32, :] = lo
         extended[8 + n, 32:48, :] = jnp.full((16, 128), there, F32).astype(BF16)
+
+
+def contact_part(cols, ex, tt, halves, extended, store):
     row = lax.broadcasted_iota(jnp.int32, (16, 128), 0)
     for b in range(PB):
         at = slice(b * BLK, (b + 1) * BLK)
-        total = None
-        for k in range(4):
-            x = extended[cols[k, b]]
-            g = dot(jnp.concatenate([x, x], axis=1), halves[b, k], NT)
-            total = g if total is None else total + g
+        picked = [extended[cols[k // 2, b]] for k in range(8)]
+        total = dot(jnp.concatenate(picked, axis=1), halves[b])
         flow = total[0:16, :] + total[16:32, :] - total[32:33, :] * tt[:, at]
         store(b, at, jnp.where(row == 15, flow + ex[b : b + 1, :], flow))
 
 
 def middle_kernel(
-    live, cols, ex_in, tt_in, ttb, halves, rxu, rxd, ryu, ryd, theta_in, there_in, edge, cell, coef, otf, slt,
-    flow, tt, theta, faces, ex, vt, xu, xd, yu, yd, extended,
+    live, cols_in, ex_in, tt_in, ttb, halves, rxu, rxd, ryu, ryd, theta_in, there_in, edge, cell, coef, otf, lists,
+    flow, tt, theta, faces, ex, vt, xu, xd, yu, yd, extended, cols, sem,
 ):
+    fetch = pltpu.make_async_copy(cols_in, cols, sem)
+    fetch.start()
     blocks = live[0] // BLK
-
-    def store(b, at, value):
-        flow[:, at] = value
-        alive = flag(b < blocks)
-        tt[:, at] = alive * (ttb[:, at] + value) + (1.0 - alive) * tt_in[:, at]
-
-    contact_part(blocks, cols, ex_in, tt_in, halves, rxu, rxd, ryu, ryd, extended, store)
-    send_ghosts(tt, slt, xu, xd, yu, yd)
+    extend(blocks, tt_in, rxu, rxd, ryu, ryd, extended)
     theta[...] = theta_in[...]
     came = ((rxd, 48, 1), (rxu, 48, 6), (ryd, 16, 3), (ryu, 16, 4))
     for f in range(4):
@@ -341,18 +346,29 @@
         face = ref[start : start + 32, :] * neighbour(n)
         faces[f * 32 : (f + 1) * 32, :] = face
         theta[FACES[f], :] = theta[FACES[f], :] + face
-    rows = jnp.concatenate(split2(faces[...].T), axis=0)
+    rows = jnp.concatenate(split2(faces[...].T), axis=1)
     there = []
     for j in range(4):
         more = pick(lane_mask(cell, j), dot(rows, otf[:, j * 256 : (j + 1) * 256]))
         there.append(pair(there_in, j) + more)
+    fetch.wait()
+
+    def store(b, at, value):
+        flow[:, at] = value
+        alive = flag(b < blocks)
+        tt[:, at] = alive * (ttb[:, at] + value) + (1.0 - alive) * tt_in[:, at]
+
+    contact_part(cols, ex_in, tt_in, halves, extended, store)
+    send_ghosts(tt, lists, xu, xd, yu, yd)
     send_faces(there, theta, edge, tt, cell, coef, blocks, otf, ex, vt, xu, xd, yu, yd)
 
 
 def last_kernel(
-    live, cols, prof, base, ex, tt, halves, rxu, rxd, ryu, ryd, strip3, strip4, prof_in, pops_in,
-    profiles, pops, extended, flow, temp, face1, face2, patch3, patch4, sems,
+    live, cols_in, prof, base, ex, tt, halves, rxu, rxd, ryu, ryd, strip3, strip4, prof_in, pops_in,
+    profiles, pops, extended, flow, temp, face1, face2, patch3, patch4, cols, sems,
 ):
+    fetch = pltpu.make_async_copy(cols_in, cols, sems.at[8])
+    fetch.start()
     blocks = live[0] // BLK
     face1[...] = rxu[48:80, :] * neighbour(6)
     face2[...] = rxd[48:80, :] * neighbour(1)
@@ -377,7 +393,9 @@
             copies.append(pltpu.make_async_copy(temp.at[two, :], profiles.at[0, two, :], sems.at[4 + b // 2]))
             copies[-1].start()
 
-    contact_part(blocks, cols, ex, tt, halves, rxu, rxd, ryu, ryd, extended, store)
+    extend(blocks, tt, rxu, rxd, ryu, ryd, extended)
+    fetch.wait()
+    contact_part(cols, ex, tt, halves, extended, store)
     for c in copies:
         c.wait()
 
@@ -414,6 +432,7 @@
     lattice = ((7, CELLS, 128), F32)
     wide = ((256, 1024), BF16)
     sends = [((80, 128), F32)] * 2 + [((48, 128), F32)] * 2
+    cols_s = pltpu.SMEM((4, PB), jnp.int32)
     ext_s = pltpu.VMEM((16, 48, 128), BF16)
 
     stay = [
@@ -426,12 +445,12 @@
             populations.reshape(7, CELLS, 128),
         )
     ]
-    cell, coef, prof, pops, ot, slt, otf, tt, theta, ex, vt, xu, xd, yu, yd = call(
+    cell, coef, lists, prof, pops, ot, otf, tt, theta, ex, vt, xu, xd, yu, yd = call(
         first_kernel, "first", (live_count, *stay),
         [SM] + [HBM] * 5,
-        [((PB, BLK), jnp.int32), lanes, ((2, SLOTS, NR), F32), lattice, ((CELLS, SLOTS), BF16), ((SLOTS, SLOTS), BF16),
-         ((128, SLOTS), BF16), shells, plane, lanes, wide] + sends,
-        scratch=[pltpu.VMEM((PB, BLK), jnp.int32), pltpu.VMEM((256, 1024), F32), pltpu.VMEM((128, 128), F32),
+        [((PB, BLK), jnp.int32), lanes, ((PB, BLK), jnp.int32), ((2, SLOTS, NR), F32), lattice, ((CELLS, SLOTS), BF16), wide,
+         shells, plane, lanes, wide] + sends,
+        scratch=[pltpu.VMEM((256, 1024), F32), pltpu.VMEM((128, 128), F32),
                  pltpu.SemaphoreType.DMA((5 + CHUNKS,))],
         us=6,
     )
@@ -439,27 +458,20 @@
     for step in range(STEPS):
         final = step == STEPS - 1
         rxu, rxd = exchange("gx", xu, xd)
-        inputs = (() if step == 0 else (faces,)) + (pops, theta, vt, ot) + (() if final else (cell,))
+        inputs = (() if step == 0 else (faces,)) + (pops, theta, vt, ot)
         if final:
             outs, specs = [lattice] + [((CX, 8, 128), F32)] * 2, [HBM, VM, VM]
             scratch = [pltpu.VMEM(*plane), pltpu.VMEM(*lattice), pltpu.SemaphoreType.DMA((CHUNKS,))]
         else:
-            outs, specs = [lattice, plane, square, lanes], None
-            scratch = [pltpu.VMEM(*plane), pltpu.VMEM(*wide)]
+            outs, specs = [lattice, plane, square], None
+            scratch = [pltpu.VMEM(*plane)]
         streamed = call(
             functools.partial(stream_kernel, final, step > 0), "stream",
-            inputs, [VM] * len(inputs), outs, out_specs=specs, scratch=scratch, us=4,
-        )
-        rxu, rxd, streamed = lax.optimization_barrier((rxu, rxd, streamed))
-        ryu, ryd = exchange(
-            "gy",
-            jnp.concatenate([yu, rxd[32:48], rxu[32:48]], axis=0),
-            jnp.concatenate([yd, rxd[0:16], rxu[0:16]], axis=0),
-        )
-        received = (rxu, rxd, ryu, ryd)
+            inputs, [VM] * len(inputs), outs, out_specs=specs, scratch=scratch, us=3,
+        )
         if step == 0:
             rc, halves = call(
-                prepare_kernel, "prepare", (rate, blocks), [VM, VM], [plane, ((PB, 4, BLK, 256), BF16)], us=1
+                prepare_kernel, "prepare", (rate, blocks), [VM, VM], [plane, ((PB, 1024, BLK), BF16)], us=1
             )
         inputs = (live_count, prof, radial, rc) + (() if step == 0 else (base, flow, conc))
         if final:
@@ -472,25 +484,38 @@
             inputs, [SM] + [VM] * (len(inputs) - 1), outs, out_specs=specs, scratch=scratch, us=1,
         )
         if final:
+            rxu, rxd, mixed = lax.optimization_barrier((rxu, rxd, mixed))
+        else:
+            rxu, rxd, streamed = lax.optimization_barrier((rxu, rxd, streamed))
+        ryu, ryd = exchange(
+            "gy",
+            jnp.concatenate([yu, rxd[32:48], rxu[32:48]], axis=0),
+            jnp.concatenate([yd, rxd[0:16], rxu[0:16]], axis=0),
+        )
+        received = (rxu, rxd, ryu, ryd)
+        if final:
             return call(
                 last_kernel, "last",
                 (live_count, cols, prof, mixed[0], ex, tt, halves, *received, *streamed[1:],
                  mixed[1], streamed[0].reshape(7, CX, 32, 128)),
-                [SM] * 2 + [VM] * 11 + [HBM] * 2,
+                [SM] + [VM] * 12 + [HBM] * 2,
                 [((2, SLOTS, NR), F32), ((7, CX, 32, 128), F32)],
                 out_specs=[HBM, HBM],
                 scratch=[ext_s, pltpu.VMEM(*shells), pltpu.VMEM(*plane)] + [pltpu.VMEM((32, 128), F32)] * 2
-                + [pltpu.VMEM((CX, 8, 128), F32)] * 2 + [pltpu.SemaphoreType.DMA((8,))],
+                + [pltpu.VMEM((CX, 8, 128), F32)] * 2 + [cols_s, pltpu.SemaphoreType.DMA((9,))],
                 aliases={13: 0, 14: 1},
             )
         base, ttb, conc = mixed
-        pops, theta, edge, there = streamed
+        pops, theta, edge = streamed
+        (there,) = call(
+            gather_kernel, "gather", (theta, ot, cell), [VM] * 3, [lanes], scratch=[pltpu.VMEM(*wide)], us=1
+        )
         flow, tt, theta, faces, ex, vt, xu, xd, yu, yd = call(
             middle_kernel, "middle",
-            (live_count, cols, ex, tt, ttb, halves, *received, theta, there, edge, cell, coef, otf, slt),
-            [SM] * 2 + [VM] * 15,
+            (live_count, cols, ex, tt, ttb, halves, *received, theta, there, edge, cell, coef, otf, lists),
+            [SM] + [VM] * 16,
             [shells, shells, plane, square, lanes, wide] + sends,
-            scratch=[ext_s],
+            scratch=[ext_s, cols_s, pltpu.SemaphoreType.DMA],
         )
 
 

time: 61.3 us -> 59.1 us (0.964)
  Pallas kernels: 23.3 us -> 20.7 us
    pallas_call x11 -> x13, Pallas kernels: 23.3 us -> 20.7 us  [call(): pl.pallas_call(kernel, name=name, out_shape=shapes, in_specs=in_specs, ou...]
  transfers between devices with their start and end apart: 12 -> 12, of which waited for: 7 -> 6; matrix products, arithmetic and copies ran while one was open for 0% -> 0% of each run, Pallas kernels for 20% -> 21%
where the time goes in v2:
time: 59.1 us
  Pallas kernels  20.7 us (35%)
  starting transfers between devices  20.4 us (35%)
  waiting for transfers between devices  16.2 us (27%)
  between operations  1.68 us (3%)
    pallas_call x13, Pallas kernels, call(): pl.pallas_call(kernel, name=name, out_shape=shapes, in_specs=in_specs, ou...  20.7 us
    ppermute x12, starting transfers between devices, exchange(): return (lax.ppermute(to_up, axis, up), lax.ppermute(to_down, axis, down))  20.4 us
    ppermute x12, waiting for transfers between devices, exchange(): return (lax.ppermute(to_up, axis, up), lax.ppermute(to_down, axis, down))  16.2 us
  transfers between devices with their start and end apart: 12, of which 6 were waited for; matrix products, arithmetic and copies ran while one was open for 0% of the time, Pallas kernels for 21%

profile of v2, /device:TPU:70, one launch (start us, length us, event | category | flops | bytes accessed | tf_op | source)
XLA Modules:
  0.0 59.1 jit_solution(5763561676514852733)
XLA Ops:
  1.3 3.5 %first.1 = (s32[8,128]{1,0:T(8,128)S(1)}, f32[8,128]{1,0:T(8,128)S(1)}, s32[8,128]{1,0:T(8,128)S(1)}, f32[2,1024,128]{2,1,0:T(8,128)S(1)}, f32[7,1024,128]{2,1,0...) custom-call(s32[1]{0:T(128)S(6)} %copy.16.live.refs_0_, ...), custom_call_target="tpu_custom_call" | custom-call | flops 600000000 | bytes 18000000 | tf_op jit(solution)/shard_map/first/pallas_call | solution.py:405
  4.8 0.0 copy-start
  4.8 0.0 copy-start.3
  4.8 4.5 %collective-permute-start = (f32[80,128]{1,0:T(8,128)S(1)}, f32[80,128]{1,0:T(8,128)S(1)}, u32[]{:S(2)}, u32[]{:S(2)}) collective-permute-start(f32[80,128]{1,0:T(8,128)S(1)} %get-tuple-element.76), channel_id=1, source_target_pairs={{0,16},{16,32},{32,48},{48,64},{64,80},{80,96},{96,112},{112,128},... | collective-permute-start | bytes 122888 | tf_op jit(solution)/shard_map/ppermute | solution.py:422
  9.3 2.2 %stream.3 = (f32[7,1024,128]{2,1,0:T(8,128)S(1)}, f32[1024,128]{1,0:T(8,128)S(1)}, f32[128,128]{1,0:T(8,128)S(1)}) custom-call(f32[7,1024,128]{2,1,0:T(8,128)S(1)} %get-tuple-element.78.refs_0_, f32[1024,128]{1,0:T(8,128)S(1)} %get-tuple-element.79.refs_1_, bf16[256,1024]{1,0:T(8,128)(2,1)S(1)} %get-tuple-element.80.refs_2_, ...), custom_call_target="tpu_custom_call" | custom-call | flops 300000000 | bytes 9000000 | tf_op jit(solution)/shard_map/stream/pallas_call | solution.py:405
  11.5 6.0 %collective-permute-done.1.rxd = f32[80,128]{1,0:T(8,128)S(1)} collective-permute-done((f32[80,128]{1,0:T(8,128)S(1)}, f32[80,128]{1,0:T(8,128)S(1)}, u32[]{:S(2)}, u32[]{:S(2)}) %collective-permute-start.1) | collective-permute-done | bytes 40992 | tf_op jit(solution)/shard_map/ppermute | solution.py:422
  17.5 0.1 collective-permute-start.2
  17.6 3.8 %collective-permute-start.3 = (f32[80,128]{1,0:T(8,128)S(1)}, f32[80,128]{1,0:T(8,128)S(1)}, u32[]{:S(2)}, u32[]{:S(2)}) collective-permute-start(f32[80,128]{1,0:T(8,128)S(1)} %pad_maximum_fusion.1), channel_id=1, source_target_pairs={{1,0},{2,1},{3,2},{4,3},{5,4},{6,5},{7,6},{8,7},{9,8},{10,9},{11,1... | collective-permute-start | bytes 122888 | tf_op jit(solution)/shard_map/ppermute | solution.py:422
  21.5 0.7 %prepare.1 = (f32[1024,128]{1,0:T(8,128)S(1)}, bf16[8,1024,128]{2,1,0:T(8,128)(2,1)S(1)}) custom-call(f32[8,128]{1,0:T(8,128)S(1)} %bitcast.9, f32[8,4,128,128]{3,2,1,0:T(8,128)S(1)} %copy-done), custom_call_target="tpu_custom_call" | custom-call | flops 100000000 | bytes 3000000 | tf_op jit(solution)/shard_map/prepare/pallas_call | solution.py:405
  22.2 0.5 mix.3
  22.8 0.8 %gather.2.there_in = f32[8,128]{1,0:T(8,128)S(1)} custom-call(f32[1024,128]{1,0:T(8,128)S(1)} %get-tuple-element.89.theta.theta_in, bf16[1024,1024]{1,0:T(8,128)(2,1)S(1)} %get-tuple-element.81.refs_3_.ot.refs_4_, s32[8,128]{1,0:T(8,128)S(1)} %get-tuple-element.90.cell), custom_call_target="tpu_custom_call" | custom-call | flops 100000000 | bytes 3000000 | tf_op jit(solution)/shard_map/gather/pallas_call | solution.py:405
  23.6 1.4 %middle.2 = (f32[16,1024]{1,0:T(8,128)S(1)}, f32[16,1024]{1,0:T(8,128)S(1)}, f32[1024,128]{1,0:T(8,128)S(1)}, f32[128,128]{1,0:T(8,128)S(1)}, f32[8,128]{1,0:T(8...) custom-call(s32[1]{0:T(128)S(6)} %copy.16.live.refs_0_, ...), custom_call_target="tpu_custom_call" | custom-call | flops 200000000 | bytes 6000000 | tf_op jit(solution)/shard_map/middle/pallas_call | solution.py:405
  25.0 0.3 collective-permute-start.4
  25.3 1.8 %collective-permute-start.5 = (f32[80,128]{1,0:T(8,128)S(1)}, f32[80,128]{1,0:T(8,128)S(1)}, u32[]{:S(2)}, u32[]{:S(2)}) collective-permute-start(f32[80,128]{1,0:T(8,128)S(1)} %get-tuple-element.102), channel_id=1, source_target_pairs={{16,0},{32,16},{48,32},{64,48},{80,64},{96,80},{112,96},{128,112},... | collective-permute-start | bytes 122888 | tf_op jit(solution)/shard_map/ppermute | solution.py:422
  27.1 2.3 %stream.4 = (f32[7,1024,128]{2,1,0:T(8,128)S(1)}, f32[1024,128]{1,0:T(8,128)S(1)}, f32[128,128]{1,0:T(8,128)S(1)}) custom-call(f32[128,128]{1,0:T(8,128)S(1)} %get-tuple-element.103.refs_0_, f32[7,1024,128]{2,1,0:T(8,128)S(1)} %get-tuple-element.104.refs_1_, f32[1024,128]{1,0:T(8,128)S(1)} %get-tuple-element.105.refs_2_, ...), custom_call_target="tpu_custom_call" | custom-call | flops 300000000 | bytes 9000000 | tf_op jit(solution)/shard_map/stream/pallas_call | solution.py:405
  29.4 4.6 %collective-permute-done.5.rxd = f32[80,128]{1,0:T(8,128)S(1)} collective-permute-done((f32[80,128]{1,0:T(8,128)S(1)}, f32[80,128]{1,0:T(8,128)S(1)}, u32[]{:S(2)}, u32[]{:S(2)}) %collective-permute-start.5) | collective-permute-done | bytes 40992 | tf_op jit(solution)/shard_map/ppermute | solution.py:422
  34.0 0.1 collective-permute-start.6
  34.1 3.8 %collective-permute-start.7 = (f32[80,128]{1,0:T(8,128)S(1)}, f32[80,128]{1,0:T(8,128)S(1)}, u32[]{:S(2)}, u32[]{:S(2)}) collective-permute-start(f32[80,128]{1,0:T(8,128)S(1)} %pad_maximum_fusion.3), channel_id=1, source_target_pairs={{1,0},{2,1},{3,2},{4,3},{5,4},{6,5},{7,6},{8,7},{9,8},{10,9},{11,1... | collective-permute-start | bytes 122888 | tf_op jit(solution)/shard_map/ppermute | solution.py:422
  37.9 0.6 mix.4
  38.5 0.8 %gather.3.there_in = f32[8,128]{1,0:T(8,128)S(1)} custom-call(f32[1024,128]{1,0:T(8,128)S(1)} %get-tuple-element.114.theta.theta_in, bf16[1024,1024]{1,0:T(8,128)(2,1)S(1)} %get-tuple-element.81.refs_3_.ot.refs_4_, s32[8,128]{1,0:T(8,128)S(1)} %get-tuple-element.90.cell), custom_call_target="tpu_custom_call" | custom-call | flops 100000000 | bytes 3000000 | tf_op jit(solution)/shard_map/gather/pallas_call | solution.py:405
  39.4 0.3 collective-permute-done.6.ryu
  39.6 0.3 collective-permute-done.7.ryd
  39.9 1.4 %middle.3 = (f32[16,1024]{1,0:T(8,128)S(1)}, f32[16,1024]{1,0:T(8,128)S(1)}, f32[1024,128]{1,0:T(8,128)S(1)}, f32[128,128]{1,0:T(8,128)S(1)}, f32[8,128]{1,0:T(8...) custom-call(s32[1]{0:T(128)S(6)} %copy.16.live.refs_0_, ...), custom_call_target="tpu_custom_call" | custom-call | flops 200000000 | bytes 6000000 | tf_op jit(solution)/shard_map/middle/pallas_call | solution.py:405
  41.2 0.1 collective-permute-start.8
  41.3 2.0 %collective-permute-start.9 = (f32[80,128]{1,0:T(8,128)S(1)}, f32[80,128]{1,0:T(8,128)S(1)}, u32[]{:S(2)}, u32[]{:S(2)}) collective-permute-start(f32[80,128]{1,0:T(8,128)S(1)} %get-tuple-element.117), channel_id=1, source_target_pairs={{16,0},{32,16},{48,32},{64,48},{80,64},{96,80},{112,96},{128,112},... | collective-permute-start | bytes 122888 | tf_op jit(solution)/shard_map/ppermute | solution.py:422
  43.3 1.2 %mix.5 = (f32[1024,128]{1,0:T(8,128)S(1)}, f32[2,1024,128]{2,1,0:T(8,128)}) custom-call(s32[1]{0:T(128)S(6)} %copy.16.live.refs_0_, f32[2,1024,128]{2,1,0:T(8,128)S(1)} %get-tuple-element.70.refs_1_.prof, f32[2,128,128]{2,1,0:T(8,128)S(1)} %copy-done.1, f32[1024,128]{1,0:T(8,128)S(1)} %get-tuple-element.73.refs_3_, ...), custom_call_target="tpu_custom_call" | custom-call | flops 100000000 | bytes 3000000 | tf_op jit(solution)/shard_map/mix/pallas_call | solution.py:405
  44.6 0.7 %collective-permute-done.8.rxu = f32[80,128]{1,0:T(8,128)S(1)} collective-permute-done((f32[80,128]{1,0:T(8,128)S(1)}, f32[80,128]{1,0:T(8,128)S(1)}, u32[]{:S(2)}, u32[]{:S(2)}) %collective-permute-start.8) | collective-permute-done | bytes 40992 | tf_op jit(solution)/shard_map/ppermute | solution.py:422
  45.3 4.3 %collective-permute-done.9.rxd = f32[80,128]{1,0:T(8,128)S(1)} collective-permute-done((f32[80,128]{1,0:T(8,128)S(1)}, f32[80,128]{1,0:T(8,128)S(1)}, u32[]{:S(2)}, u32[]{:S(2)}) %collective-permute-start.9) | collective-permute-done | bytes 40992 | tf_op jit(solution)/shard_map/ppermute | solution.py:422
  49.6 0.1 collective-permute-start.10
  49.7 3.8 %collective-permute-start.11 = (f32[80,128]{1,0:T(8,128)S(1)}, f32[80,128]{1,0:T(8,128)S(1)}, u32[]{:S(2)}, u32[]{:S(2)}) collective-permute-start(f32[80,128]{1,0:T(8,128)S(1)} %pad_maximum_fusion.5), channel_id=1, source_target_pairs={{1,0},{2,1},{3,2},{4,3},{5,4},{6,5},{7,6},{8,7},{9,8},{10,9},{11,1... | collective-permute-start | bytes 122888 | tf_op jit(solution)/shard_map/ppermute | solution.py:422
  53.6 3.4 %stream.5 = (f32[7,1024,128]{2,1,0:T(8,128)}, f32[32,8,128]{2,1,0:T(8,128)S(1)}, f32[32,8,128]{2,1,0:T(8,128)S(1)}) custom-call(f32[128,128]{1,0:T(8,128)S(1)} %get-tuple-element.130.refs_0_, f32[7,1024,128]{2,1,0:T(8,128)S(1)} %get-tuple-element.131.refs_1_, f32[1024,128]{1,0:T(8,128)S(1)} %get-tuple-element.132.refs_2_, ...), custom_call_target="tpu_custom_call" | custom-call | flops 300000000 | bytes 9000000 | tf_op jit(solution)/shard_map/stream/pallas_call | solution.py:405
  57.0 1.9 %last.1 = (f32[2,1024,128]{2,1,0:T(8,128)}, f32[7,32,32,128]{3,2,1,0:T(8,128)}) custom-call(s32[1]{0:T(128)S(6)} %copy.16.live.refs_0_, s32[4,8]{1,0:T(4,128)S(1)} %bitcast.8, f32[2,1024,128]{2,1,0:T(8,128)S(1)} %get-tuple-element.70.refs_1_.prof, f32[1024,128]{1,0:T(8,128)S(1)} %get-tuple-element.123.base, ...), custom_call_target="tpu_custom_call", output_to_operand_aliasing={{0}: (13, {}), {1}: (14, {})} | custom-call | flops 200000000 | bytes 6000000 | tf_op jit(solution)/shard_map/last/pallas_call | solution.py:405
  (24 shorter events, 0.1 us)
Async XLA Ops:
  4.8 16.7 %copy-start = (f32[8,4,128,128]{3,2,1,0:T(8,128)S(1)}, f32[8,4,128,128]{3,2,1,0:T(8,128)}, u32[]{:S(2)}) copy-start(f32[8,4,128,128]{3,2,1,0:T(8,128)} %blocks.1) | copy-start | bytes 6291460
  4.8 16.7 %copy-start.3 = (f32[1024]{0:T(1024)S(1)}, f32[1024]{0:T(1024)}, u32[]{:S(2)}) copy-start(f32[1024]{0:T(1024)} %param.12) | copy-start | bytes 12292
  4.8 6.7 %collective-permute-start = (f32[80,128]{1,0:T(8,128)S(1)}, f32[80,128]{1,0:T(8,128)S(1)}, u32[]{:S(2)}, u32[]{:S(2)}) collective-permute-start(f32[80,128]{1,0:T(8,128)S(1)} %get-tuple-element.76), channel_id=1, source_target_pairs={{0,16},{16,32},{32,48},{48,64},{64,80},{80,96},{96,112},{112,128},... | collective-permute-start | bytes 122888 | tf_op jit(solution)/shard_map/ppermute | solution.py:422
  9.3 8.2 %collective-permute-start.1 = (f32[80,128]{1,0:T(8,128)S(1)}, f32[80,128]{1,0:T(8,128)S(1)}, u32[]{:S(2)}, u32[]{:S(2)}) collective-permute-start(f32[80,128]{1,0:T(8,128)S(1)} %get-tuple-element.77), channel_id=1, source_target_pairs={{16,0},{32,16},{48,32},{64,48},{80,64},{96,80},{112,96},{128,112},... | collective-permute-start | bytes 122888 | tf_op jit(solution)/shard_map/ppermute | solution.py:422
  9.3 12.9 %copy-start.1 = (f32[2,128,128]{2,1,0:T(8,128)S(1)}, f32[2,128,128]{2,1,0:T(8,128)}, u32[]{:S(2)}) copy-start(f32[2,128,128]{2,1,0:T(8,128)} %refs_2_.5) | copy-start | bytes 393220
  11.5 12.1 %copy-start.2 = (s32[8,4]{0,1:T(4,128)S(1)}, s32[8,4]{0,1:T(4,128)}, u32[]{:S(2)}) copy-start(s32[8,4]{0,1:T(4,128)} %param.17) | copy-start | bytes 388
  17.5 6.0 %collective-permute-start.2 = (f32[80,128]{1,0:T(8,128)S(1)}, f32[80,128]{1,0:T(8,128)S(1)}, u32[]{:S(2)}, u32[]{:S(2)}) collective-permute-start(f32[80,128]{1,0:T(8,128)S(1)} %pad_maximum_fusion), channel_id=1, source_target_pairs={{0,1},{1,2},{2,3},{3,4},{4,5},{5,6},{6,7},{7,8},{8,9},{9,10},{10,1... | collective-permute-start | bytes 122888 | tf_op jit(solution)/shard_map/ppermute | solution.py:422
  17.6 5.9 %collective-permute-start.3 = (f32[80,128]{1,0:T(8,128)S(1)}, f32[80,128]{1,0:T(8,128)S(1)}, u32[]{:S(2)}, u32[]{:S(2)}) collective-permute-start(f32[80,128]{1,0:T(8,128)S(1)} %pad_maximum_fusion.1), channel_id=1, source_target_pairs={{1,0},{2,1},{3,2},{4,3},{5,4},{6,5},{7,6},{8,7},{9,8},{10,9},{11,1... | collective-permute-start | bytes 122888 | tf_op jit(solution)/shard_map/ppermute | solution.py:422
  25.0 4.4 %collective-permute-start.4 = (f32[80,128]{1,0:T(8,128)S(1)}, f32[80,128]{1,0:T(8,128)S(1)}, u32[]{:S(2)}, u32[]{:S(2)}) collective-permute-start(f32[80,128]{1,0:T(8,128)S(1)} %get-tuple-element.101), channel_id=1, source_target_pairs={{0,16},{16,32},{32,48},{48,64},{64,80},{80,96},{96,112},{112,128},... | collective-permute-start | bytes 122888 | tf_op jit(solution)/shard_map/ppermute | solution.py:422
  25.3 8.7 %collective-permute-start.5 = (f32[80,128]{1,0:T(8,128)S(1)}, f32[80,128]{1,0:T(8,128)S(1)}, u32[]{:S(2)}, u32[]{:S(2)}) collective-permute-start(f32[80,128]{1,0:T(8,128)S(1)} %get-tuple-element.102), channel_id=1, source_target_pairs={{16,0},{32,16},{48,32},{64,48},{80,64},{96,80},{112,96},{128,112},... | collective-permute-start | bytes 122888 | tf_op jit(solution)/shard_map/ppermute | solution.py:422
  34.0 5.6 %collective-permute-start.6 = (f32[80,128]{1,0:T(8,128)S(1)}, f32[80,128]{1,0:T(8,128)S(1)}, u32[]{:S(2)}, u32[]{:S(2)}) collective-permute-start(f32[80,128]{1,0:T(8,128)S(1)} %pad_maximum_fusion.2), channel_id=1, source_target_pairs={{0,1},{1,2},{2,3},{3,4},{4,5},{5,6},{6,7},{7,8},{8,9},{9,10},{10,1... | collective-permute-start | bytes 122888 | tf_op jit(solution)/shard_map/ppermute | solution.py:422
  34.1 5.8 %collective-permute-start.7 = (f32[80,128]{1,0:T(8,128)S(1)}, f32[80,128]{1,0:T(8,128)S(1)}, u32[]{:S(2)}, u32[]{:S(2)}) collective-permute-start(f32[80,128]{1,0:T(8,128)S(1)} %pad_maximum_fusion.3), channel_id=1, source_target_pairs={{1,0},{2,1},{3,2},{4,3},{5,4},{6,5},{7,6},{8,7},{9,8},{10,9},{11,1... | collective-permute-start | bytes 122888 | tf_op jit(solution)/shard_map/ppermute | solution.py:422
  41.2 4.1 %collective-permute-start.8 = (f32[80,128]{1,0:T(8,128)S(1)}, f32[80,128]{1,0:T(8,128)S(1)}, u32[]{:S(2)}, u32[]{:S(2)}) collective-permute-start(f32[80,128]{1,0:T(8,128)S(1)} %get-tuple-element.116), channel_id=1, source_target_pairs={{0,16},{16,32},{32,48},{48,64},{64,80},{80,96},{96,112},{112,128},... | collective-permute-start | bytes 122888 | tf_op jit(solution)/shard_map/ppermute | solution.py:422
  41.3 8.3 %collective-permute-start.9 = (f32[80,128]{1,0:T(8,128)S(1)}, f32[80,128]{1,0:T(8,128)S(1)}, u32[]{:S(2)}, u32[]{:S(2)}) collective-permute-start(f32[80,128]{1,0:T(8,128)S(1)} %get-tuple-element.117), channel_id=1, source_target_pairs={{16,0},{32,16},{48,32},{64,48},{80,64},{96,80},{112,96},{128,112},... | collective-permute-start | bytes 122888 | tf_op jit(solution)/shard_map/ppermute | solution.py:422
  49.6 7.4 %collective-permute-start.10 = (f32[80,128]{1,0:T(8,128)S(1)}, f32[80,128]{1,0:T(8,128)S(1)}, u32[]{:S(2)}, u32[]{:S(2)}) collective-permute-start(f32[80,128]{1,0:T(8,128)S(1)} %pad_maximum_fusion.4), channel_id=1, source_target_pairs={{0,1},{1,2},{2,3},{3,4},{4,5},{5,6},{6,7},{7,8},{8,9},{9,10},{10,1... | collective-permute-start | bytes 122888 | tf_op jit(solution)/shard_map/ppermute | solution.py:422
  49.7 7.3 %collective-permute-start.11 = (f32[80,128]{1,0:T(8,128)S(1)}, f32[80,128]{1,0:T(8,128)S(1)}, u32[]{:S(2)}, u32[]{:S(2)}) collective-permute-start(f32[80,128]{1,0:T(8,128)S(1)} %pad_maximum_fusion.5), channel_id=1, source_target_pairs={{1,0},{2,1},{3,2},{4,3},{5,4},{6,5},{7,6},{8,7},{9,8},{10,9},{11,1... | collective-permute-start | bytes 122888 | tf_op jit(solution)/shard_map/ppermute | solution.py:422

commit v3 on v2

--- a/solution.py
+++ b/solution.py
@@ -115,7 +115,7 @@
 def first_kernel(
     live, cell_in, coef_in, lists_in, prof_in, pops_in,
     cell, coef, lists, prof, pops, ot, otf, tt, theta, ex, vt, xu, xd, yu, yd,
-    gathered, edge, sems,
+    gathered, rows, edge, sems,
 ):
     blocks = live[0] // BLK
     copies = [
@@ -124,8 +124,8 @@
         pltpu.make_async_copy(prof_in.at[0], prof.at[0], sems.at[2]),
     ]
     for c in range(CHUNKS):
-        rows = pl.ds(c * CHUNK, CHUNK)
-        copies.append(pltpu.make_async_copy(pops_in.at[:, rows, :], pops.at[:, rows, :], sems.at[3 + c]))
+        part = pl.ds(c * CHUNK, CHUNK)
+        copies.append(pltpu.make_async_copy(pops_in.at[:, part, :], pops.at[:, part, :], sems.at[3 + c]))
     copies.append(pltpu.make_async_copy(coef_in, coef, sems.at[3 + CHUNKS]))
     copies.append(pltpu.make_async_copy(prof_in.at[1], prof.at[1], sems.at[4 + CHUNKS]))
     for c in copies:
@@ -149,26 +149,27 @@
     send_ghosts(tt, lists, xu, xd, yu, yd)
     for c in range(CHUNKS):
         copies[3 + c].wait()
-        parts = []
         for h in range(CHUNK // 128):
             at = slice(c * CHUNK + h * 128, c * CHUNK + (h + 1) * 128)
             total = pops[0, at, :]
             for i in range(1, 7):
                 total = total + pops[i, at, :]
             theta[at, :] = total
-            parts.append(jnp.concatenate(split2(total.T), axis=0))
-        rows = jnp.concatenate(parts, axis=1)
-        for j in range(4):
-            at = slice(j * 256, (j + 1) * 256)
-            g = dot(rows, ot[c * CHUNK : (c + 1) * CHUNK, at])
-            gathered[:, at] = g if c == 0 else gathered[:, at] + g
+            hi, lo = split2(total.T)
+            rows[0:128, at] = hi
+            rows[128:256, at] = lo
+        if c == CHUNKS - 2:
+            for j in range(4):
+                at = slice(j * 256, (j + 1) * 256)
+                gathered[:, at] = dot(rows[:, 0 : (c + 1) * CHUNK], ot[0 : (c + 1) * CHUNK, at])
     for i in range(4):
         edge[i * 32 : (i + 1) * 32, :] = pops[i + 1, FACES[i], :]
     copies[3 + CHUNKS].wait()
     there = []
     for j in range(4):
         at = slice(j * 256, (j + 1) * 256)
-        there.append(pick(lane_mask(cell, j), gathered[0:128, at] + gathered[128:256, at]))
+        g = gathered[:, at] + dot(rows[:, CELLS - CHUNK :], ot[CELLS - CHUNK :, at])
+        there.append(pick(lane_mask(cell, j), g[0:128, :] + g[128:256, :]))
     send_faces(there, theta, edge, tt, cell, coef, blocks, otf, ex, vt, xu, xd, yu, yd)
     copies[4 + CHUNKS].wait()
 
@@ -177,7 +178,7 @@
     if has_faces:
         faces, refs = refs[0], refs[1:]
     if last:
-        pops, theta, vt, ot, out, strip3, strip4, source, new, sems = refs
+        pops, theta, vt, ot, new, source = refs
     else:
         pops, theta, vt, ot, new, theta_new, edge, source = refs
     for j in range(4):
@@ -222,21 +223,11 @@
                 if not last:
                     theta_new[at, :] = theta_new[at, :] - 0.25 * face
 
-    copies = []
     for c in range(CHUNKS):
         lax.fori_loop(c * 8, (c + 1) * 8, row, 0, unroll=2)
         if has_faces:
             carry_faces(c)
-        if last:
-            at = pl.ds(c * CHUNK, CHUNK)
-            copies.append(pltpu.make_async_copy(new.at[:, at, :], out.at[:, at, :], sems.at[c]))
-            copies[-1].start()
-            for x in range(c * 8, (c + 1) * 8):
-                strip3[x] = new[3, x * 32 : x * 32 + 8, :]
-                strip4[x] = new[4, x * 32 + 24 : x * 32 + 32, :]
     if last:
-        for copy in copies:
-            copy.wait()
         return
     for i in range(4):
         edge[i * 32 : (i + 1) * 32, :] = new[i + 1, FACES[i], :]
@@ -274,7 +265,7 @@
     else:
         live, prof, radial, rc, base_in, flow, conc_in, *refs = refs
     if last:
-        base, out, conc_new, sems = refs
+        pops, base, out, lattice, conc_new, sems = refs
     else:
         base, ttb, conc_new = refs
     blocks = live[0] // BLK
@@ -284,6 +275,13 @@
         top = jnp.concatenate([hi, lo], axis=1)
         wide.append(jnp.concatenate([top, jnp.concatenate([hi, jnp.zeros_like(hi)], axis=1)], axis=0))
     copies = []
+    if last:
+        parts = [(0, slice(0, CX), 0, 32), (1, slice(1, CX), 0, 32), (2, slice(0, CX - 1), 0, 32)]
+        parts += [(3, slice(0, CX), 8, 32), (4, slice(0, CX), 0, 24), (5, slice(0, CX), 0, 32), (6, slice(0, CX), 0, 32)]
+        for n, (i, x, y0, y1) in enumerate(parts):
+            at = pl.ds(x.start, x.stop - x.start), pl.ds(y0, y1 - y0)
+            copies.append(pltpu.make_async_copy(pops.at[i, *at, :], lattice.at[i, *at, :], sems.at[4 + n]))
+            copies[-1].start()
     for b in range(PB):
         at = slice(b * BLK, (b + 1) * BLK)
         conc = prof[1, at, :] if first else conc_in[at, :]
@@ -364,7 +362,7 @@
 
 
 def last_kernel(
-    live, cols_in, prof, base, ex, tt, halves, rxu, rxd, ryu, ryd, strip3, strip4, prof_in, pops_in,
+    live, cols_in, prof, base, ex, tt, halves, rxu, rxd, ryu, ryd, new, prof_in, pops_in,
     profiles, pops, extended, flow, temp, face1, face2, patch3, patch4, cols, sems,
 ):
     fetch = pltpu.make_async_copy(cols_in, cols, sems.at[8])
@@ -374,8 +372,8 @@
     face2[...] = rxd[48:80, :] * neighbour(1)
     y = lax.broadcasted_iota(jnp.int32, (8, 128), 0)
     for x in range(CX):
-        patch3[x] = jnp.where(y == 0, ryu[16 + x : 17 + x, :] * neighbour(4), strip3[x])
-        patch4[x] = jnp.where(y == 7, ryd[16 + x : 17 + x, :] * neighbour(3), strip4[x])
+        patch3[x] = jnp.where(y == 0, ryu[16 + x : 17 + x, :] * neighbour(4), new[3, x, 0:8, :])
+        patch4[x] = jnp.where(y == 7, ryd[16 + x : 17 + x, :] * neighbour(3), new[4, x, 24:32, :])
     copies = [
         pltpu.make_async_copy(face1, pops.at[1, 0], sems.at[0]),
         pltpu.make_async_copy(face2, pops.at[2, CX - 1], sems.at[1]),
@@ -450,7 +448,7 @@
         [SM] + [HBM] * 5,
         [((PB, BLK), jnp.int32), lanes, ((PB, BLK), jnp.int32), ((2, SLOTS, NR), F32), lattice, ((CELLS, SLOTS), BF16), wide,
          shells, plane, lanes, wide] + sends,
-        scratch=[pltpu.VMEM((256, 1024), F32), pltpu.VMEM((128, 128), F32),
+        scratch=[pltpu.VMEM((256, 1024), F32), pltpu.VMEM(*wide), pltpu.VMEM((128, 128), F32),
                  pltpu.SemaphoreType.DMA((5 + CHUNKS,))],
         us=6,
     )
@@ -459,15 +457,16 @@
         final = step == STEPS - 1
         rxu, rxd = exchange("gx", xu, xd)
         inputs = (() if step == 0 else (faces,)) + (pops, theta, vt, ot)
-        if final:
-            outs, specs = [lattice] + [((CX, 8, 128), F32)] * 2, [HBM, VM, VM]
-            scratch = [pltpu.VMEM(*plane), pltpu.VMEM(*lattice), pltpu.SemaphoreType.DMA((CHUNKS,))]
-        else:
-            outs, specs = [lattice, plane, square], None
-            scratch = [pltpu.VMEM(*plane)]
+        outs = [lattice] if final else [lattice, plane, square]
         streamed = call(
             functools.partial(stream_kernel, final, step > 0), "stream",
-            inputs, [VM] * len(inputs), outs, out_specs=specs, scratch=scratch, us=3,
+            inputs, [VM] * len(inputs), outs, scratch=[pltpu.VMEM(*plane)], us=3,
+        )
+        rxu, rxd, streamed = lax.optimization_barrier((rxu, rxd, streamed))
+        ryu, ryd = exchange(
+            "gy",
+            jnp.concatenate([yu, rxd[32:48], rxu[32:48]], axis=0),
+            jnp.concatenate([yd, rxd[0:16], rxu[0:16]], axis=0),
         )
         if step == 0:
             rc, halves = call(
@@ -475,35 +474,28 @@
             )
         inputs = (live_count, prof, radial, rc) + (() if step == 0 else (base, flow, conc))
         if final:
-            outs, specs = [plane, ((2, SLOTS, NR), F32)], [VM, HBM]
-            scratch = [pltpu.VMEM(*plane), pltpu.SemaphoreType.DMA((4,))]
+            streamed = [streamed[0].reshape(7, CX, 32, 128)]
+            inputs = (*inputs, *streamed)
+            outs, specs = [plane, ((2, SLOTS, NR), F32), ((7, CX, 32, 128), F32)], [VM, HBM, HBM]
+            scratch = [pltpu.VMEM(*plane), pltpu.SemaphoreType.DMA((11,))]
         else:
             outs, specs, scratch = [plane, shells, plane], None, []
         mixed = call(
             functools.partial(mix_kernel, step == 0, final), "mix",
             inputs, [SM] + [VM] * (len(inputs) - 1), outs, out_specs=specs, scratch=scratch, us=1,
         )
-        if final:
-            rxu, rxd, mixed = lax.optimization_barrier((rxu, rxd, mixed))
-        else:
-            rxu, rxd, streamed = lax.optimization_barrier((rxu, rxd, streamed))
-        ryu, ryd = exchange(
-            "gy",
-            jnp.concatenate([yu, rxd[32:48], rxu[32:48]], axis=0),
-            jnp.concatenate([yd, rxd[0:16], rxu[0:16]], axis=0),
-        )
         received = (rxu, rxd, ryu, ryd)
         if final:
             return call(
                 last_kernel, "last",
-                (live_count, cols, prof, mixed[0], ex, tt, halves, *received, *streamed[1:],
-                 mixed[1], streamed[0].reshape(7, CX, 32, 128)),
-                [SM] + [VM] * 12 + [HBM] * 2,
+                (live_count, cols, prof, mixed[0], ex, tt, halves, *received, *streamed,
+                 mixed[1], mixed[2]),
+                [SM] + [VM] * 11 + [HBM] * 2,
                 [((2, SLOTS, NR), F32), ((7, CX, 32, 128), F32)],
                 out_specs=[HBM, HBM],
                 scratch=[ext_s, pltpu.VMEM(*shells), pltpu.VMEM(*plane)] + [pltpu.VMEM((32, 128), F32)] * 2
                 + [pltpu.VMEM((CX, 8, 128), F32)] * 2 + [cols_s, pltpu.SemaphoreType.DMA((9,))],
-                aliases={13: 0, 14: 1},
+                aliases={12: 0, 13: 1},
             )
         base, ttb, conc = mixed
         pops, theta, edge = streamed

time: 59.1 us -> 57.8 us (0.978)
  waiting for transfers between devices: 16.2 us -> 15 us
    ppermute x12, waiting for transfers between devices: 16.2 us -> 15 us  [exchange(): return (lax.ppermute(to_up, axis, up), lax.ppermute(to_down, axis, down))]
  transfers between devices with their start and end apart: 12 -> 12, of which waited for: 6 -> 5; matrix products, arithmetic and copies ran while one was open for 0% -> 0% of each run, Pallas kernels for 21% -> 21%
where the time goes in v3:
time: 57.8 us; the launch traced here: 57.7 us
  Pallas kernels  20.5 us (35%)
  starting transfers between devices  20.4 us (35%)
  waiting for transfers between devices  15 us (26%)
  between operations  1.69 us (3%)
    pallas_call x13, Pallas kernels, call(): pl.pallas_call(kernel, name=name, out_shape=shapes, in_specs=in_specs, ou...  20.5 us
    ppermute x12, starting transfers between devices, exchange(): return (lax.ppermute(to_up, axis, up), lax.ppermute(to_down, axis, down))  20.4 us
    ppermute x12, waiting for transfers between devices, exchange(): return (lax.ppermute(to_up, axis, up), lax.ppermute(to_down, axis, down))  15 us
  transfers between devices with their start and end apart: 12, of which 5 were waited for; matrix products, arithmetic and copies ran while one was open for 0% of the time, Pallas kernels for 21%

profile of v3, /device:TPU:70, one launch (start us, length us, event | category | flops | bytes accessed | tf_op | source)
XLA Modules:
  0.0 57.7 jit_solution(17555229356643236300)
XLA Ops:
  1.3 3.5 %first.1 = (s32[8,128]{1,0:T(8,128)S(1)}, f32[8,128]{1,0:T(8,128)S(1)}, s32[8,128]{1,0:T(8,128)S(1)}, f32[2,1024,128]{2,1,0:T(8,128)S(1)}, f32[7,1024,128]{2,1,0...) custom-call(s32[1]{0:T(128)S(6)} %copy.16.live.refs_0_, ...), custom_call_target="tpu_custom_call" | custom-call | flops 600000000 | bytes 18000000 | tf_op jit(solution)/shard_map/first/pallas_call | solution.py:403
  4.8 0.0 copy-start
  4.8 0.0 copy-start.3
  4.9 4.5 %collective-permute-start = (f32[80,128]{1,0:T(8,128)S(1)}, f32[80,128]{1,0:T(8,128)S(1)}, u32[]{:S(2)}, u32[]{:S(2)}) collective-permute-start(f32[80,128]{1,0:T(8,128)S(1)} %get-tuple-element.74), channel_id=1, source_target_pairs={{0,16},{16,32},{32,48},{48,64},{64,80},{80,96},{96,112},{112,128},... | collective-permute-start | bytes 122888 | tf_op jit(solution)/shard_map/ppermute | solution.py:420
  9.3 2.2 %stream.3 = (f32[7,1024,128]{2,1,0:T(8,128)S(1)}, f32[1024,128]{1,0:T(8,128)S(1)}, f32[128,128]{1,0:T(8,128)S(1)}) custom-call(f32[7,1024,128]{2,1,0:T(8,128)S(1)} %get-tuple-element.76.refs_0_, f32[1024,128]{1,0:T(8,128)S(1)} %get-tuple-element.77.refs_1_, bf16[256,1024]{1,0:T(8,128)(2,1)S(1)} %get-tuple-element.78.refs_2_, ...), custom_call_target="tpu_custom_call" | custom-call | flops 300000000 | bytes 9000000 | tf_op jit(solution)/shard_map/stream/pallas_call | solution.py:403
  11.6 0.0 copy-start.2
  11.6 6.0 %collective-permute-done.1.rxd = f32[80,128]{1,0:T(8,128)S(1)} collective-permute-done((f32[80,128]{1,0:T(8,128)S(1)}, f32[80,128]{1,0:T(8,128)S(1)}, u32[]{:S(2)}, u32[]{:S(2)}) %collective-permute-start.1) | collective-permute-done | bytes 40992 | tf_op jit(solution)/shard_map/ppermute | solution.py:420
  17.6 0.1 collective-permute-start.2
  17.7 3.8 %collective-permute-start.3 = (f32[80,128]{1,0:T(8,128)S(1)}, f32[80,128]{1,0:T(8,128)S(1)}, u32[]{:S(2)}, u32[]{:S(2)}) collective-permute-start(f32[80,128]{1,0:T(8,128)S(1)} %pad_maximum_fusion.1), channel_id=1, source_target_pairs={{1,0},{2,1},{3,2},{4,3},{5,4},{6,5},{7,6},{8,7},{9,8},{10,9},{11,1... | collective-permute-start | bytes 122888 | tf_op jit(solution)/shard_map/ppermute | solution.py:420
  21.5 0.7 %prepare.1 = (f32[1024,128]{1,0:T(8,128)S(1)}, bf16[8,1024,128]{2,1,0:T(8,128)(2,1)S(1)}) custom-call(f32[8,128]{1,0:T(8,128)S(1)} %bitcast.11, f32[8,4,128,128]{3,2,1,0:T(8,128)S(1)} %copy-done), custom_call_target="tpu_custom_call" | custom-call | flops 100000000 | bytes 3000000 | tf_op jit(solution)/shard_map/prepare/pallas_call | solution.py:403
  22.3 0.5 mix.3
  22.8 0.8 %gather.2.there_in = f32[8,128]{1,0:T(8,128)S(1)} custom-call(f32[1024,128]{1,0:T(8,128)S(1)} %get-tuple-element.87.theta.theta_in, bf16[1024,1024]{1,0:T(8,128)(2,1)S(1)} %get-tuple-element.79.refs_3_.ot.refs_4_, s32[8,128]{1,0:T(8,128)S(1)} %get-tuple-element.88.cell), custom_call_target="tpu_custom_call" | custom-call | flops 100000000 | bytes 3000000 | tf_op jit(solution)/shard_map/gather/pallas_call | solution.py:403
  23.6 1.4 %middle.2 = (f32[16,1024]{1,0:T(8,128)S(1)}, f32[16,1024]{1,0:T(8,128)S(1)}, f32[1024,128]{1,0:T(8,128)S(1)}, f32[128,128]{1,0:T(8,128)S(1)}, f32[8,128]{1,0:T(8...) custom-call(s32[1]{0:T(128)S(6)} %copy.16.live.refs_0_, ...), custom_call_target="tpu_custom_call" | custom-call | flops 200000000 | bytes 6000000 | tf_op jit(solution)/shard_map/middle/pallas_call | solution.py:403
  25.0 0.4 collective-permute-start.4
  25.4 1.7 %collective-permute-start.5 = (f32[80,128]{1,0:T(8,128)S(1)}, f32[80,128]{1,0:T(8,128)S(1)}, u32[]{:S(2)}, u32[]{:S(2)}) collective-permute-start(f32[80,128]{1,0:T(8,128)S(1)} %get-tuple-element.100), channel_id=1, source_target_pairs={{16,0},{32,16},{48,32},{64,48},{80,64},{96,80},{112,96},{128,112},... | collective-permute-start | bytes 122888 | tf_op jit(solution)/shard_map/ppermute | solution.py:420
  27.1 2.3 %stream.4 = (f32[7,1024,128]{2,1,0:T(8,128)S(1)}, f32[1024,128]{1,0:T(8,128)S(1)}, f32[128,128]{1,0:T(8,128)S(1)}) custom-call(f32[128,128]{1,0:T(8,128)S(1)} %get-tuple-element.101.refs_0_, f32[7,1024,128]{2,1,0:T(8,128)S(1)} %get-tuple-element.102.refs_1_, f32[1024,128]{1,0:T(8,128)S(1)} %get-tuple-element.103.refs_2_, ...), custom_call_target="tpu_custom_call" | custom-call | flops 300000000 | bytes 9000000 | tf_op jit(solution)/shard_map/stream/pallas_call | solution.py:403
  29.4 4.6 %collective-permute-done.5.rxd = f32[80,128]{1,0:T(8,128)S(1)} collective-permute-done((f32[80,128]{1,0:T(8,128)S(1)}, f32[80,128]{1,0:T(8,128)S(1)}, u32[]{:S(2)}, u32[]{:S(2)}) %collective-permute-start.5) | collective-permute-done | bytes 40992 | tf_op jit(solution)/shard_map/ppermute | solution.py:420
  34.1 0.1 collective-permute-start.6
  34.2 3.8 %collective-permute-start.7 = (f32[80,128]{1,0:T(8,128)S(1)}, f32[80,128]{1,0:T(8,128)S(1)}, u32[]{:S(2)}, u32[]{:S(2)}) collective-permute-start(f32[80,128]{1,0:T(8,128)S(1)} %pad_maximum_fusion.3), channel_id=1, source_target_pairs={{1,0},{2,1},{3,2},{4,3},{5,4},{6,5},{7,6},{8,7},{9,8},{10,9},{11,1... | collective-permute-start | bytes 122888 | tf_op jit(solution)/shard_map/ppermute | solution.py:420
  38.0 0.6 %mix.4 = (f32[1024,128]{1,0:T(8,128)S(1)}, f32[16,1024]{1,0:T(8,128)S(1)}, f32[1024,128]{1,0:T(8,128)S(1)}) custom-call(s32[1]{0:T(128)S(6)} %copy.16.live.refs_0_, f32[2,1024,128]{2,1,0:T(8,128)S(1)} %get-tuple-element.67.refs_1_.prof, f32[2,128,128]{2,1,0:T(8,128)S(1)} %copy-done.1, f32[1024,128]{1,0:T(8,128)S(1)} %get-tuple-element.68.refs_3_, ...), custom_call_target="tpu_custom_call" | custom-call | flops 100000000 | bytes 3000000 | tf_op jit(solution)/shard_map/mix/pallas_call | solution.py:403
  38.6 0.8 %gather.3.there_in = f32[8,128]{1,0:T(8,128)S(1)} custom-call(f32[1024,128]{1,0:T(8,128)S(1)} %get-tuple-element.112.theta.theta_in, bf16[1024,1024]{1,0:T(8,128)(2,1)S(1)} %get-tuple-element.79.refs_3_.ot.refs_4_, s32[8,128]{1,0:T(8,128)S(1)} %get-tuple-element.88.cell), custom_call_target="tpu_custom_call" | custom-call | flops 100000000 | bytes 3000000 | tf_op jit(solution)/shard_map/gather/pallas_call | solution.py:403
  39.4 0.3 collective-permute-done.6.ryu
  39.7 0.3 collective-permute-done.7.ryd
  40.0 1.4 %middle.3 = (f32[16,1024]{1,0:T(8,128)S(1)}, f32[16,1024]{1,0:T(8,128)S(1)}, f32[1024,128]{1,0:T(8,128)S(1)}, f32[128,128]{1,0:T(8,128)S(1)}, f32[8,128]{1,0:T(8...) custom-call(s32[1]{0:T(128)S(6)} %copy.16.live.refs_0_, ...), custom_call_target="tpu_custom_call" | custom-call | flops 200000000 | bytes 6000000 | tf_op jit(solution)/shard_map/middle/pallas_call | solution.py:403
  41.3 0.1 collective-permute-start.8
  41.4 2.0 %collective-permute-start.9 = (f32[80,128]{1,0:T(8,128)S(1)}, f32[80,128]{1,0:T(8,128)S(1)}, u32[]{:S(2)}, u32[]{:S(2)}) collective-permute-start(f32[80,128]{1,0:T(8,128)S(1)} %get-tuple-element.117), channel_id=1, source_target_pairs={{16,0},{32,16},{48,32},{64,48},{80,64},{96,80},{112,96},{128,112},... | collective-permute-start | bytes 122888 | tf_op jit(solution)/shard_map/ppermute | solution.py:420
  43.4 2.4 %stream.5 = f32[7,1024,128]{2,1,0:T(8,128)S(1)} custom-call(f32[128,128]{1,0:T(8,128)S(1)} %get-tuple-element.118.refs_0_, f32[7,1024,128]{2,1,0:T(8,128)S(1)} %get-tuple-element.119.refs_1_, f32[1024,128]{1,0:T(8,128)S(1)} %get-tuple-element.120.refs_2_, bf16[256,1024]{1,0:T(8,128)(2,1)S(1)} %get-tuple-element.121.refs_3_, ...), custom_call_target="tpu_custom_call" | custom-call | flops 300000000 | bytes 9000000 | tf_op jit(solution)/shard_map/stream/pallas_call | solution.py:403
  45.9 3.9 %collective-permute-done.9.rxd = f32[80,128]{1,0:T(8,128)S(1)} collective-permute-done((f32[80,128]{1,0:T(8,128)S(1)}, f32[80,128]{1,0:T(8,128)S(1)}, u32[]{:S(2)}, u32[]{:S(2)}) %collective-permute-start.9) | collective-permute-done | bytes 40992 | tf_op jit(solution)/shard_map/ppermute | solution.py:420
  49.7 0.1 collective-permute-start.10
  49.9 3.8 %collective-permute-start.11 = (f32[80,128]{1,0:T(8,128)S(1)}, f32[80,128]{1,0:T(8,128)S(1)}, u32[]{:S(2)}, u32[]{:S(2)}) collective-permute-start(f32[80,128]{1,0:T(8,128)S(1)} %pad_maximum_fusion.5), channel_id=1, source_target_pairs={{1,0},{2,1},{3,2},{4,3},{5,4},{6,5},{7,6},{8,7},{9,8},{10,9},{11,1... | collective-permute-start | bytes 122888 | tf_op jit(solution)/shard_map/ppermute | solution.py:420
  53.7 2.0 %mix.5 = (f32[1024,128]{1,0:T(8,128)S(1)}, f32[2,1024,128]{2,1,0:T(8,128)}, f32[7,32,32,128]{3,2,1,0:T(8,128)}) custom-call(s32[1]{0:T(128)S(6)} %copy.16.live.refs_0_, f32[2,1024,128]{2,1,0:T(8,128)S(1)} %get-tuple-element.67.refs_1_.prof, f32[2,128,128]{2,1,0:T(8,128)S(1)} %copy-done.1, f32[1024,128]{1,0:T(8,128)S(1)} %get-tuple-element.68.refs_3_, ...), custom_call_target="tpu_custom_call" | custom-call | flops 100000000 | bytes 3000000 | tf_op jit(solution)/shard_map/mix/pallas_call | solution.py:403
  55.7 1.9 %last.1 = (f32[2,1024,128]{2,1,0:T(8,128)}, f32[7,32,32,128]{3,2,1,0:T(8,128)}) custom-call(s32[1]{0:T(128)S(6)} %copy.16.live.refs_0_, s32[4,8]{1,0:T(4,128)S(1)} %bitcast.10, f32[2,1024,128]{2,1,0:T(8,128)S(1)} %get-tuple-element.67.refs_1_.prof, f32[1024,128]{1,0:T(8,128)S(1)} %get-tuple-element.123.base, ...), custom_call_target="tpu_custom_call", output_to_operand_aliasing={{0}: (12, {}), {1}: (13, {})} | custom-call | flops 200000000 | bytes 6000000 | tf_op jit(solution)/shard_map/last/pallas_call | solution.py:403
  (24 shorter events, 0.1 us)
Async XLA Ops:
  4.8 16.7 %copy-start = (f32[8,4,128,128]{3,2,1,0:T(8,128)S(1)}, f32[8,4,128,128]{3,2,1,0:T(8,128)}, u32[]{:S(2)}) copy-start(f32[8,4,128,128]{3,2,1,0:T(8,128)} %blocks.1) | copy-start | bytes 6291460
  4.8 16.7 %copy-start.3 = (f32[1024]{0:T(1024)S(1)}, f32[1024]{0:T(1024)}, u32[]{:S(2)}) copy-start(f32[1024]{0:T(1024)} %param.12) | copy-start | bytes 12292
  4.9 6.7 %collective-permute-start = (f32[80,128]{1,0:T(8,128)S(1)}, f32[80,128]{1,0:T(8,128)S(1)}, u32[]{:S(2)}, u32[]{:S(2)}) collective-permute-start(f32[80,128]{1,0:T(8,128)S(1)} %get-tuple-element.74), channel_id=1, source_target_pairs={{0,16},{16,32},{32,48},{48,64},{64,80},{80,96},{96,112},{112,128},... | collective-permute-start | bytes 122888 | tf_op jit(solution)/shard_map/ppermute | solution.py:420
  9.3 8.2 %collective-permute-start.1 = (f32[80,128]{1,0:T(8,128)S(1)}, f32[80,128]{1,0:T(8,128)S(1)}, u32[]{:S(2)}, u32[]{:S(2)}) collective-permute-start(f32[80,128]{1,0:T(8,128)S(1)} %get-tuple-element.75), channel_id=1, source_target_pairs={{16,0},{32,16},{48,32},{64,48},{80,64},{96,80},{112,96},{128,112},... | collective-permute-start | bytes 122888 | tf_op jit(solution)/shard_map/ppermute | solution.py:420
  9.3 12.9 %copy-start.1 = (f32[2,128,128]{2,1,0:T(8,128)S(1)}, f32[2,128,128]{2,1,0:T(8,128)}, u32[]{:S(2)}) copy-start(f32[2,128,128]{2,1,0:T(8,128)} %refs_2_.5) | copy-start | bytes 393220
  11.6 12.1 %copy-start.2 = (s32[8,4]{0,1:T(4,128)S(1)}, s32[8,4]{0,1:T(4,128)}, u32[]{:S(2)}) copy-start(s32[8,4]{0,1:T(4,128)} %param.17) | copy-start | bytes 388
  17.6 6.0 %collective-permute-start.2 = (f32[80,128]{1,0:T(8,128)S(1)}, f32[80,128]{1,0:T(8,128)S(1)}, u32[]{:S(2)}, u32[]{:S(2)}) collective-permute-start(f32[80,128]{1,0:T(8,128)S(1)} %pad_maximum_fusion), channel_id=1, source_target_pairs={{0,1},{1,2},{2,3},{3,4},{4,5},{5,6},{6,7},{7,8},{8,9},{9,10},{10,1... | collective-permute-start | bytes 122888 | tf_op jit(solution)/shard_map/ppermute | solution.py:420
  17.7 5.9 %collective-permute-start.3 = (f32[80,128]{1,0:T(8,128)S(1)}, f32[80,128]{1,0:T(8,128)S(1)}, u32[]{:S(2)}, u32[]{:S(2)}) collective-permute-start(f32[80,128]{1,0:T(8,128)S(1)} %pad_maximum_fusion.1), channel_id=1, source_target_pairs={{1,0},{2,1},{3,2},{4,3},{5,4},{6,5},{7,6},{8,7},{9,8},{10,9},{11,1... | collective-permute-start | bytes 122888 | tf_op jit(solution)/shard_map/ppermute | solution.py:420
  25.0 4.4 %collective-permute-start.4 = (f32[80,128]{1,0:T(8,128)S(1)}, f32[80,128]{1,0:T(8,128)S(1)}, u32[]{:S(2)}, u32[]{:S(2)}) collective-permute-start(f32[80,128]{1,0:T(8,128)S(1)} %get-tuple-element.99), channel_id=1, source_target_pairs={{0,16},{16,32},{32,48},{48,64},{64,80},{80,96},{96,112},{112,128},... | collective-permute-start | bytes 122888 | tf_op jit(solution)/shard_map/ppermute | solution.py:420
  25.4 8.7 %collective-permute-start.5 = (f32[80,128]{1,0:T(8,128)S(1)}, f32[80,128]{1,0:T(8,128)S(1)}, u32[]{:S(2)}, u32[]{:S(2)}) collective-permute-start(f32[80,128]{1,0:T(8,128)S(1)} %get-tuple-element.100), channel_id=1, source_target_pairs={{16,0},{32,16},{48,32},{64,48},{80,64},{96,80},{112,96},{128,112},... | collective-permute-start | bytes 122888 | tf_op jit(solution)/shard_map/ppermute | solution.py:420
  34.1 5.6 %collective-permute-start.6 = (f32[80,128]{1,0:T(8,128)S(1)}, f32[80,128]{1,0:T(8,128)S(1)}, u32[]{:S(2)}, u32[]{:S(2)}) collective-permute-start(f32[80,128]{1,0:T(8,128)S(1)} %pad_maximum_fusion.2), channel_id=1, source_target_pairs={{0,1},{1,2},{2,3},{3,4},{4,5},{5,6},{6,7},{7,8},{8,9},{9,10},{10,1... | collective-permute-start | bytes 122888 | tf_op jit(solution)/shard_map/ppermute | solution.py:420
  34.2 5.8 %collective-permute-start.7 = (f32[80,128]{1,0:T(8,128)S(1)}, f32[80,128]{1,0:T(8,128)S(1)}, u32[]{:S(2)}, u32[]{:S(2)}) collective-permute-start(f32[80,128]{1,0:T(8,128)S(1)} %pad_maximum_fusion.3), channel_id=1, source_target_pairs={{1,0},{2,1},{3,2},{4,3},{5,4},{6,5},{7,6},{8,7},{9,8},{10,9},{11,1... | collective-permute-start | bytes 122888 | tf_op jit(solution)/shard_map/ppermute | solution.py:420
  41.3 4.5 %collective-permute-start.8 = (f32[80,128]{1,0:T(8,128)S(1)}, f32[80,128]{1,0:T(8,128)S(1)}, u32[]{:S(2)}, u32[]{:S(2)}) collective-permute-start(f32[80,128]{1,0:T(8,128)S(1)} %get-tuple-element.116), channel_id=1, source_target_pairs={{0,16},{16,32},{32,48},{48,64},{64,80},{80,96},{96,112},{112,128},... | collective-permute-start | bytes 122888 | tf_op jit(solution)/shard_map/ppermute | solution.py:420
  41.4 8.3 %collective-permute-start.9 = (f32[80,128]{1,0:T(8,128)S(1)}, f32[80,128]{1,0:T(8,128)S(1)}, u32[]{:S(2)}, u32[]{:S(2)}) collective-permute-start(f32[80,128]{1,0:T(8,128)S(1)} %get-tuple-element.117), channel_id=1, source_target_pairs={{16,0},{32,16},{48,32},{64,48},{80,64},{96,80},{112,96},{128,112},... | collective-permute-start | bytes 122888 | tf_op jit(solution)/shard_map/ppermute | solution.py:420
  49.7 5.9 %collective-permute-start.10 = (f32[80,128]{1,0:T(8,128)S(1)}, f32[80,128]{1,0:T(8,128)S(1)}, u32[]{:S(2)}, u32[]{:S(2)}) collective-permute-start(f32[80,128]{1,0:T(8,128)S(1)} %pad_maximum_fusion.4), channel_id=1, source_target_pairs={{0,1},{1,2},{2,3},{3,4},{4,5},{5,6},{6,7},{7,8},{8,9},{9,10},{10,1... | collective-permute-start | bytes 122888 | tf_op jit(solution)/shard_map/ppermute | solution.py:420
  49.9 5.8 %collective-permute-start.11 = (f32[80,128]{1,0:T(8,128)S(1)}, f32[80,128]{1,0:T(8,128)S(1)}, u32[]{:S(2)}, u32[]{:S(2)}) collective-permute-start(f32[80,128]{1,0:T(8,128)S(1)} %pad_maximum_fusion.5), channel_id=1, source_target_pairs={{1,0},{2,1},{3,2},{4,3},{5,4},{6,5},{7,6},{8,7},{9,8},{10,9},{11,1... | collective-permute-start | bytes 122888 | tf_op jit(solution)/shard_map/ppermute | solution.py:420

commit v4 on v3

--- a/solution.py
+++ b/solution.py
@@ -17,6 +17,7 @@
 CELLS = 1024
 CHUNKS = 4
 CHUNK = CELLS // CHUNKS
+PARTS = ((0, 512), (512, 1024))
 F32 = jnp.float32
 BF16 = jnp.bfloat16
 
@@ -123,11 +124,11 @@
         pltpu.make_async_copy(lists_in, lists, sems.at[1]),
         pltpu.make_async_copy(prof_in.at[0], prof.at[0], sems.at[2]),
     ]
-    for c in range(CHUNKS):
-        part = pl.ds(c * CHUNK, CHUNK)
+    for c, (start, stop) in enumerate(PARTS):
+        part = pl.ds(start, stop - start)
         copies.append(pltpu.make_async_copy(pops_in.at[:, part, :], pops.at[:, part, :], sems.at[3 + c]))
-    copies.append(pltpu.make_async_copy(coef_in, coef, sems.at[3 + CHUNKS]))
-    copies.append(pltpu.make_async_copy(prof_in.at[1], prof.at[1], sems.at[4 + CHUNKS]))
+    copies.append(pltpu.make_async_copy(coef_in, coef, sems.at[3 + len(PARTS)]))
+    copies.append(pltpu.make_async_copy(prof_in.at[1], prof.at[1], sems.at[4 + len(PARTS)]))
     for c in copies:
         c.start()
     sub = lax.broadcasted_iota(jnp.int32, (CELLS, BLK), 0)
@@ -147,10 +148,10 @@
         at = slice(b * BLK, (b + 1) * BLK)
         tt[:, at] = prof[0, at, :].T[NR - SHELL :, :]
     send_ghosts(tt, lists, xu, xd, yu, yd)
-    for c in range(CHUNKS):
+    for c, (start, stop) in enumerate(PARTS):
         copies[3 + c].wait()
-        for h in range(CHUNK // 128):
-            at = slice(c * CHUNK + h * 128, c * CHUNK + (h + 1) * 128)
+        for h in range(start, stop, 128):
+            at = slice(h, h + 128)
             total = pops[0, at, :]
             for i in range(1, 7):
                 total = total + pops[i, at, :]
@@ -158,20 +159,20 @@
             hi, lo = split2(total.T)
             rows[0:128, at] = hi
             rows[128:256, at] = lo
-        if c == CHUNKS - 2:
+        if stop < CELLS:
             for j in range(4):
                 at = slice(j * 256, (j + 1) * 256)
-                gathered[:, at] = dot(rows[:, 0 : (c + 1) * CHUNK], ot[0 : (c + 1) * CHUNK, at])
+                gathered[:, at] = dot(rows[:, 0:stop], ot[0:stop, at])
     for i in range(4):
         edge[i * 32 : (i + 1) * 32, :] = pops[i + 1, FACES[i], :]
-    copies[3 + CHUNKS].wait()
+    copies[3 + len(PARTS)].wait()
     there = []
     for j in range(4):
         at = slice(j * 256, (j + 1) * 256)
-        g = gathered[:, at] + dot(rows[:, CELLS - CHUNK :], ot[CELLS - CHUNK :, at])
+        g = gathered[:, at] + dot(rows[:, PARTS[-1][0] :], ot[PARTS[-1][0] :, at])
         there.append(pick(lane_mask(cell, j), g[0:128, :] + g[128:256, :]))
     send_faces(there, theta, edge, tt, cell, coef, blocks, otf, ex, vt, xu, xd, yu, yd)
-    copies[4 + CHUNKS].wait()
+    copies[4 + len(PARTS)].wait()
 
 
 def stream_kernel(last, has_faces, *refs):
@@ -449,7 +450,7 @@
         [((PB, BLK), jnp.int32), lanes, ((PB, BLK), jnp.int32), ((2, SLOTS, NR), F32), lattice, ((CELLS, SLOTS), BF16), wide,
          shells, plane, lanes, wide] + sends,
         scratch=[pltpu.VMEM((256, 1024), F32), pltpu.VMEM(*wide), pltpu.VMEM((128, 128), F32),
-                 pltpu.SemaphoreType.DMA((5 + CHUNKS,))],
+                 pltpu.SemaphoreType.DMA((5 + len(PARTS),))],
         us=6,
     )
     faces = base = flow = conc = there = edge = None

time: 57.8 us -> 57.6 us (level)
  transfers between devices with their start and end apart: 12 -> 12, of which waited for: 5 -> 5; matrix products, arithmetic and copies ran while one was open for 0% -> 0% of each run, Pallas kernels for 21% -> 22%
where the time goes in v4:
time: 57.6 us; the launch traced here: 57.5 us
  starting transfers between devices  20.4 us (35%)
  Pallas kernels  20.3 us (35%)
  waiting for transfers between devices  15 us (26%)
  between operations  1.69 us (3%)
    ppermute x12, starting transfers between devices, exchange(): return (lax.ppermute(to_up, axis, up), lax.ppermute(to_down, axis, down))  20.4 us
    pallas_call x13, Pallas kernels, call(): pl.pallas_call(kernel, name=name, out_shape=shapes, in_specs=in_specs, ou...  20.3 us
    ppermute x12, waiting for transfers between devices, exchange(): return (lax.ppermute(to_up, axis, up), lax.ppermute(to_down, axis, down))  15 us
  transfers between devices with their start and end apart: 12, of which 5 were waited for; matrix products, arithmetic and copies ran while one was open for 0% of the time, Pallas kernels for 22%

profile of v4, /device:TPU:70, one launch (start us, length us, event | category | flops | bytes accessed | tf_op | source)
XLA Modules:
  0.0 57.5 jit_solution(18413151364796734457)
XLA Ops:
  1.3 3.3 %first.1 = (s32[8,128]{1,0:T(8,128)S(1)}, f32[8,128]{1,0:T(8,128)S(1)}, s32[8,128]{1,0:T(8,128)S(1)}, f32[2,1024,128]{2,1,0:T(8,128)S(1)}, f32[7,1024,128]{2,1,0...) custom-call(s32[1]{0:T(128)S(6)} %copy.16.live.refs_0_, ...), custom_call_target="tpu_custom_call" | custom-call | flops 600000000 | bytes 18000000 | tf_op jit(solution)/shard_map/first/pallas_call | solution.py:404
  4.6 0.0 copy-start
  4.6 0.0 copy-start.3
  4.6 4.5 %collective-permute-start = (f32[80,128]{1,0:T(8,128)S(1)}, f32[80,128]{1,0:T(8,128)S(1)}, u32[]{:S(2)}, u32[]{:S(2)}) collective-permute-start(f32[80,128]{1,0:T(8,128)S(1)} %get-tuple-element.74), channel_id=1, source_target_pairs={{0,16},{16,32},{32,48},{48,64},{64,80},{80,96},{96,112},{112,128},... | collective-permute-start | bytes 122888 | tf_op jit(solution)/shard_map/ppermute | solution.py:421
  9.1 2.2 %stream.3 = (f32[7,1024,128]{2,1,0:T(8,128)S(1)}, f32[1024,128]{1,0:T(8,128)S(1)}, f32[128,128]{1,0:T(8,128)S(1)}) custom-call(f32[7,1024,128]{2,1,0:T(8,128)S(1)} %get-tuple-element.76.refs_0_, f32[1024,128]{1,0:T(8,128)S(1)} %get-tuple-element.77.refs_1_, bf16[256,1024]{1,0:T(8,128)(2,1)S(1)} %get-tuple-element.78.refs_2_, ...), custom_call_target="tpu_custom_call" | custom-call | flops 300000000 | bytes 9000000 | tf_op jit(solution)/shard_map/stream/pallas_call | solution.py:404
  11.4 0.0 copy-start.2
  11.4 6.0 %collective-permute-done.1.rxd = f32[80,128]{1,0:T(8,128)S(1)} collective-permute-done((f32[80,128]{1,0:T(8,128)S(1)}, f32[80,128]{1,0:T(8,128)S(1)}, u32[]{:S(2)}, u32[]{:S(2)}) %collective-permute-start.1) | collective-permute-done | bytes 40992 | tf_op jit(solution)/shard_map/ppermute | solution.py:421
  17.4 0.1 collective-permute-start.2
  17.5 3.8 %collective-permute-start.3 = (f32[80,128]{1,0:T(8,128)S(1)}, f32[80,128]{1,0:T(8,128)S(1)}, u32[]{:S(2)}, u32[]{:S(2)}) collective-permute-start(f32[80,128]{1,0:T(8,128)S(1)} %pad_maximum_fusion.1), channel_id=1, source_target_pairs={{1,0},{2,1},{3,2},{4,3},{5,4},{6,5},{7,6},{8,7},{9,8},{10,9},{11,1... | collective-permute-start | bytes 122888 | tf_op jit(solution)/shard_map/ppermute | solution.py:421
  21.3 0.7 %prepare.1 = (f32[1024,128]{1,0:T(8,128)S(1)}, bf16[8,1024,128]{2,1,0:T(8,128)(2,1)S(1)}) custom-call(f32[8,128]{1,0:T(8,128)S(1)} %bitcast.11, f32[8,4,128,128]{3,2,1,0:T(8,128)S(1)} %copy-done), custom_call_target="tpu_custom_call" | custom-call | flops 100000000 | bytes 3000000 | tf_op jit(solution)/shard_map/prepare/pallas_call | solution.py:404
  22.1 0.5 mix.3
  22.6 0.8 %gather.2.there_in = f32[8,128]{1,0:T(8,128)S(1)} custom-call(f32[1024,128]{1,0:T(8,128)S(1)} %get-tuple-element.87.theta.theta_in, bf16[1024,1024]{1,0:T(8,128)(2,1)S(1)} %get-tuple-element.79.refs_3_.ot.refs_4_, s32[8,128]{1,0:T(8,128)S(1)} %get-tuple-element.88.cell), custom_call_target="tpu_custom_call" | custom-call | flops 100000000 | bytes 3000000 | tf_op jit(solution)/shard_map/gather/pallas_call | solution.py:404
  23.4 1.4 %middle.2 = (f32[16,1024]{1,0:T(8,128)S(1)}, f32[16,1024]{1,0:T(8,128)S(1)}, f32[1024,128]{1,0:T(8,128)S(1)}, f32[128,128]{1,0:T(8,128)S(1)}, f32[8,128]{1,0:T(8...) custom-call(s32[1]{0:T(128)S(6)} %copy.16.live.refs_0_, ...), custom_call_target="tpu_custom_call" | custom-call | flops 200000000 | bytes 6000000 | tf_op jit(solution)/shard_map/middle/pallas_call | solution.py:404
  24.8 0.4 collective-permute-start.4
  25.2 1.7 %collective-permute-start.5 = (f32[80,128]{1,0:T(8,128)S(1)}, f32[80,128]{1,0:T(8,128)S(1)}, u32[]{:S(2)}, u32[]{:S(2)}) collective-permute-start(f32[80,128]{1,0:T(8,128)S(1)} %get-tuple-element.100), channel_id=1, source_target_pairs={{16,0},{32,16},{48,32},{64,48},{80,64},{96,80},{112,96},{128,112},... | collective-permute-start | bytes 122888 | tf_op jit(solution)/shard_map/ppermute | solution.py:421
  26.9 2.3 %stream.4 = (f32[7,1024,128]{2,1,0:T(8,128)S(1)}, f32[1024,128]{1,0:T(8,128)S(1)}, f32[128,128]{1,0:T(8,128)S(1)}) custom-call(f32[128,128]{1,0:T(8,128)S(1)} %get-tuple-element.101.refs_0_, f32[7,1024,128]{2,1,0:T(8,128)S(1)} %get-tuple-element.102.refs_1_, f32[1024,128]{1,0:T(8,128)S(1)} %get-tuple-element.103.refs_2_, ...), custom_call_target="tpu_custom_call" | custom-call | flops 300000000 | bytes 9000000 | tf_op jit(solution)/shard_map/stream/pallas_call | solution.py:404
  29.2 4.6 %collective-permute-done.5.rxd = f32[80,128]{1,0:T(8,128)S(1)} collective-permute-done((f32[80,128]{1,0:T(8,128)S(1)}, f32[80,128]{1,0:T(8,128)S(1)}, u32[]{:S(2)}, u32[]{:S(2)}) %collective-permute-start.5) | collective-permute-done | bytes 40992 | tf_op jit(solution)/shard_map/ppermute | solution.py:421
  33.9 0.1 collective-permute-start.6
  34.0 3.8 %collective-permute-start.7 = (f32[80,128]{1,0:T(8,128)S(1)}, f32[80,128]{1,0:T(8,128)S(1)}, u32[]{:S(2)}, u32[]{:S(2)}) collective-permute-start(f32[80,128]{1,0:T(8,128)S(1)} %pad_maximum_fusion.3), channel_id=1, source_target_pairs={{1,0},{2,1},{3,2},{4,3},{5,4},{6,5},{7,6},{8,7},{9,8},{10,9},{11,1... | collective-permute-start | bytes 122888 | tf_op jit(solution)/shard_map/ppermute | solution.py:421
  37.8 0.6 %mix.4 = (f32[1024,128]{1,0:T(8,128)S(1)}, f32[16,1024]{1,0:T(8,128)S(1)}, f32[1024,128]{1,0:T(8,128)S(1)}) custom-call(s32[1]{0:T(128)S(6)} %copy.16.live.refs_0_, f32[2,1024,128]{2,1,0:T(8,128)S(1)} %get-tuple-element.67.refs_1_.prof, f32[2,128,128]{2,1,0:T(8,128)S(1)} %copy-done.1, f32[1024,128]{1,0:T(8,128)S(1)} %get-tuple-element.68.refs_3_, ...), custom_call_target="tpu_custom_call" | custom-call | flops 100000000 | bytes 3000000 | tf_op jit(solution)/shard_map/mix/pallas_call | solution.py:404
  38.4 0.8 %gather.3.there_in = f32[8,128]{1,0:T(8,128)S(1)} custom-call(f32[1024,128]{1,0:T(8,128)S(1)} %get-tuple-element.112.theta.theta_in, bf16[1024,1024]{1,0:T(8,128)(2,1)S(1)} %get-tuple-element.79.refs_3_.ot.refs_4_, s32[8,128]{1,0:T(8,128)S(1)} %get-tuple-element.88.cell), custom_call_target="tpu_custom_call" | custom-call | flops 100000000 | bytes 3000000 | tf_op jit(solution)/shard_map/gather/pallas_call | solution.py:404
  39.2 0.3 collective-permute-done.6.ryu
  39.5 0.2 collective-permute-done.7.ryd
  39.7 1.4 %middle.3 = (f32[16,1024]{1,0:T(8,128)S(1)}, f32[16,1024]{1,0:T(8,128)S(1)}, f32[1024,128]{1,0:T(8,128)S(1)}, f32[128,128]{1,0:T(8,128)S(1)}, f32[8,128]{1,0:T(8...) custom-call(s32[1]{0:T(128)S(6)} %copy.16.live.refs_0_, ...), custom_call_target="tpu_custom_call" | custom-call | flops 200000000 | bytes 6000000 | tf_op jit(solution)/shard_map/middle/pallas_call | solution.py:404
  41.1 0.1 collective-permute-start.8
  41.2 2.0 %collective-permute-start.9 = (f32[80,128]{1,0:T(8,128)S(1)}, f32[80,128]{1,0:T(8,128)S(1)}, u32[]{:S(2)}, u32[]{:S(2)}) collective-permute-start(f32[80,128]{1,0:T(8,128)S(1)} %get-tuple-element.117), channel_id=1, source_target_pairs={{16,0},{32,16},{48,32},{64,48},{80,64},{96,80},{112,96},{128,112},... | collective-permute-start | bytes 122888 | tf_op jit(solution)/shard_map/ppermute | solution.py:421
  43.2 2.4 %stream.5 = f32[7,1024,128]{2,1,0:T(8,128)S(1)} custom-call(f32[128,128]{1,0:T(8,128)S(1)} %get-tuple-element.118.refs_0_, f32[7,1024,128]{2,1,0:T(8,128)S(1)} %get-tuple-element.119.refs_1_, f32[1024,128]{1,0:T(8,128)S(1)} %get-tuple-element.120.refs_2_, bf16[256,1024]{1,0:T(8,128)(2,1)S(1)} %get-tuple-element.121.refs_3_, ...), custom_call_target="tpu_custom_call" | custom-call | flops 300000000 | bytes 9000000 | tf_op jit(solution)/shard_map/stream/pallas_call | solution.py:404
  45.6 3.9 %collective-permute-done.9.rxd = f32[80,128]{1,0:T(8,128)S(1)} collective-permute-done((f32[80,128]{1,0:T(8,128)S(1)}, f32[80,128]{1,0:T(8,128)S(1)}, u32[]{:S(2)}, u32[]{:S(2)}) %collective-permute-start.9) | collective-permute-done | bytes 40992 | tf_op jit(solution)/shard_map/ppermute | solution.py:421
  49.5 0.1 collective-permute-start.10
  49.6 3.8 %collective-permute-start.11 = (f32[80,128]{1,0:T(8,128)S(1)}, f32[80,128]{1,0:T(8,128)S(1)}, u32[]{:S(2)}, u32[]{:S(2)}) collective-permute-start(f32[80,128]{1,0:T(8,128)S(1)} %pad_maximum_fusion.5), channel_id=1, source_target_pairs={{1,0},{2,1},{3,2},{4,3},{5,4},{6,5},{7,6},{8,7},{9,8},{10,9},{11,1... | collective-permute-start | bytes 122888 | tf_op jit(solution)/shard_map/ppermute | solution.py:421
  53.4 2.0 %mix.5 = (f32[1024,128]{1,0:T(8,128)S(1)}, f32[2,1024,128]{2,1,0:T(8,128)}, f32[7,32,32,128]{3,2,1,0:T(8,128)}) custom-call(s32[1]{0:T(128)S(6)} %copy.16.live.refs_0_, f32[2,1024,128]{2,1,0:T(8,128)S(1)} %get-tuple-element.67.refs_1_.prof, f32[2,128,128]{2,1,0:T(8,128)S(1)} %copy-done.1, f32[1024,128]{1,0:T(8,128)S(1)} %get-tuple-element.68.refs_3_, ...), custom_call_target="tpu_custom_call" | custom-call | flops 100000000 | bytes 3000000 | tf_op jit(solution)/shard_map/mix/pallas_call | solution.py:404
  55.5 1.9 %last.1 = (f32[2,1024,128]{2,1,0:T(8,128)}, f32[7,32,32,128]{3,2,1,0:T(8,128)}) custom-call(s32[1]{0:T(128)S(6)} %copy.16.live.refs_0_, s32[4,8]{1,0:T(4,128)S(1)} %bitcast.10, f32[2,1024,128]{2,1,0:T(8,128)S(1)} %get-tuple-element.67.refs_1_.prof, f32[1024,128]{1,0:T(8,128)S(1)} %get-tuple-element.123.base, ...), custom_call_target="tpu_custom_call", output_to_operand_aliasing={{0}: (12, {}), {1}: (13, {})} | custom-call | flops 200000000 | bytes 6000000 | tf_op jit(solution)/shard_map/last/pallas_call | solution.py:404
  (24 shorter events, 0.1 us)
Async XLA Ops:
  4.6 16.7 %copy-start = (f32[8,4,128,128]{3,2,1,0:T(8,128)S(1)}, f32[8,4,128,128]{3,2,1,0:T(8,128)}, u32[]{:S(2)}) copy-start(f32[8,4,128,128]{3,2,1,0:T(8,128)} %blocks.1) | copy-start | bytes 6291460
  4.6 16.7 %copy-start.3 = (f32[1024]{0:T(1024)S(1)}, f32[1024]{0:T(1024)}, u32[]{:S(2)}) copy-start(f32[1024]{0:T(1024)} %param.12) | copy-start | bytes 12292
  4.6 6.7 %collective-permute-start = (f32[80,128]{1,0:T(8,128)S(1)}, f32[80,128]{1,0:T(8,128)S(1)}, u32[]{:S(2)}, u32[]{:S(2)}) collective-permute-start(f32[80,128]{1,0:T(8,128)S(1)} %get-tuple-element.74), channel_id=1, source_target_pairs={{0,16},{16,32},{32,48},{48,64},{64,80},{80,96},{96,112},{112,128},... | collective-permute-start | bytes 122888 | tf_op jit(solution)/shard_map/ppermute | solution.py:421
  9.1 8.2 %collective-permute-start.1 = (f32[80,128]{1,0:T(8,128)S(1)}, f32[80,128]{1,0:T(8,128)S(1)}, u32[]{:S(2)}, u32[]{:S(2)}) collective-permute-start(f32[80,128]{1,0:T(8,128)S(1)} %get-tuple-element.75), channel_id=1, source_target_pairs={{16,0},{32,16},{48,32},{64,48},{80,64},{96,80},{112,96},{128,112},... | collective-permute-start | bytes 122888 | tf_op jit(solution)/shard_map/ppermute | solution.py:421
  9.1 12.9 %copy-start.1 = (f32[2,128,128]{2,1,0:T(8,128)S(1)}, f32[2,128,128]{2,1,0:T(8,128)}, u32[]{:S(2)}) copy-start(f32[2,128,128]{2,1,0:T(8,128)} %refs_2_.5) | copy-start | bytes 393220
  11.4 12.1 %copy-start.2 = (s32[8,4]{0,1:T(4,128)S(1)}, s32[8,4]{0,1:T(4,128)}, u32[]{:S(2)}) copy-start(s32[8,4]{0,1:T(4,128)} %param.17) | copy-start | bytes 388
  17.4 6.0 %collective-permute-start.2 = (f32[80,128]{1,0:T(8,128)S(1)}, f32[80,128]{1,0:T(8,128)S(1)}, u32[]{:S(2)}, u32[]{:S(2)}) collective-permute-start(f32[80,128]{1,0:T(8,128)S(1)} %pad_maximum_fusion), channel_id=1, source_target_pairs={{0,1},{1,2},{2,3},{3,4},{4,5},{5,6},{6,7},{7,8},{8,9},{9,10},{10,1... | collective-permute-start | bytes 122888 | tf_op jit(solution)/shard_map/ppermute | solution.py:421
  17.5 5.9 %collective-permute-start.3 = (f32[80,128]{1,0:T(8,128)S(1)}, f32[80,128]{1,0:T(8,128)S(1)}, u32[]{:S(2)}, u32[]{:S(2)}) collective-permute-start(f32[80,128]{1,0:T(8,128)S(1)} %pad_maximum_fusion.1), channel_id=1, source_target_pairs={{1,0},{2,1},{3,2},{4,3},{5,4},{6,5},{7,6},{8,7},{9,8},{10,9},{11,1... | collective-permute-start | bytes 122888 | tf_op jit(solution)/shard_map/ppermute | solution.py:421
  24.8 4.4 %collective-permute-start.4 = (f32[80,128]{1,0:T(8,128)S(1)}, f32[80,128]{1,0:T(8,128)S(1)}, u32[]{:S(2)}, u32[]{:S(2)}) collective-permute-start(f32[80,128]{1,0:T(8,128)S(1)} %get-tuple-element.99), channel_id=1, source_target_pairs={{0,16},{16,32},{32,48},{48,64},{64,80},{80,96},{96,112},{112,128},... | collective-permute-start | bytes 122888 | tf_op jit(solution)/shard_map/ppermute | solution.py:421
  25.2 8.7 %collective-permute-start.5 = (f32[80,128]{1,0:T(8,128)S(1)}, f32[80,128]{1,0:T(8,128)S(1)}, u32[]{:S(2)}, u32[]{:S(2)}) collective-permute-start(f32[80,128]{1,0:T(8,128)S(1)} %get-tuple-element.100), channel_id=1, source_target_pairs={{16,0},{32,16},{48,32},{64,48},{80,64},{96,80},{112,96},{128,112},... | collective-permute-start | bytes 122888 | tf_op jit(solution)/shard_map/ppermute | solution.py:421
  33.9 5.6 %collective-permute-start.6 = (f32[80,128]{1,0:T(8,128)S(1)}, f32[80,128]{1,0:T(8,128)S(1)}, u32[]{:S(2)}, u32[]{:S(2)}) collective-permute-start(f32[80,128]{1,0:T(8,128)S(1)} %pad_maximum_fusion.2), channel_id=1, source_target_pairs={{0,1},{1,2},{2,3},{3,4},{4,5},{5,6},{6,7},{7,8},{8,9},{9,10},{10,1... | collective-permute-start | bytes 122888 | tf_op jit(solution)/shard_map/ppermute | solution.py:421
  34.0 5.7 %collective-permute-start.7 = (f32[80,128]{1,0:T(8,128)S(1)}, f32[80,128]{1,0:T(8,128)S(1)}, u32[]{:S(2)}, u32[]{:S(2)}) collective-permute-start(f32[80,128]{1,0:T(8,128)S(1)} %pad_maximum_fusion.3), channel_id=1, source_target_pairs={{1,0},{2,1},{3,2},{4,3},{5,4},{6,5},{7,6},{8,7},{9,8},{10,9},{11,1... | collective-permute-start | bytes 122888 | tf_op jit(solution)/shard_map/ppermute | solution.py:421
  41.1 4.5 %collective-permute-start.8 = (f32[80,128]{1,0:T(8,128)S(1)}, f32[80,128]{1,0:T(8,128)S(1)}, u32[]{:S(2)}, u32[]{:S(2)}) collective-permute-start(f32[80,128]{1,0:T(8,128)S(1)} %get-tuple-element.116), channel_id=1, source_target_pairs={{0,16},{16,32},{32,48},{48,64},{64,80},{80,96},{96,112},{112,128},... | collective-permute-start | bytes 122888 | tf_op jit(solution)/shard_map/ppermute | solution.py:421
  41.2 8.3 %collective-permute-start.9 = (f32[80,128]{1,0:T(8,128)S(1)}, f32[80,128]{1,0:T(8,128)S(1)}, u32[]{:S(2)}, u32[]{:S(2)}) collective-permute-start(f32[80,128]{1,0:T(8,128)S(1)} %get-tuple-element.117), channel_id=1, source_target_pairs={{16,0},{32,16},{48,32},{64,48},{80,64},{96,80},{112,96},{128,112},... | collective-permute-start | bytes 122888 | tf_op jit(solution)/shard_map/ppermute | solution.py:421
  49.5 5.9 %collective-permute-start.10 = (f32[80,128]{1,0:T(8,128)S(1)}, f32[80,128]{1,0:T(8,128)S(1)}, u32[]{:S(2)}, u32[]{:S(2)}) collective-permute-start(f32[80,128]{1,0:T(8,128)S(1)} %pad_maximum_fusion.4), channel_id=1, source_target_pairs={{0,1},{1,2},{2,3},{3,4},{4,5},{5,6},{6,7},{7,8},{8,9},{9,10},{10,1... | collective-permute-start | bytes 122888 | tf_op jit(solution)/shard_map/ppermute | solution.py:421
  49.6 5.8 %collective-permute-start.11 = (f32[80,128]{1,0:T(8,128)S(1)}, f32[80,128]{1,0:T(8,128)S(1)}, u32[]{:S(2)}, u32[]{:S(2)}) collective-permute-start(f32[80,128]{1,0:T(8,128)S(1)} %pad_maximum_fusion.5), channel_id=1, source_target_pairs={{1,0},{2,1},{3,2},{4,3},{5,4},{6,5},{7,6},{8,7},{9,8},{10,9},{11,1... | collective-permute-start | bytes 122888 | tf_op jit(solution)/shard_map/ppermute | solution.py:421
